TPU v7x, 32 devices: a whole 2x2x4 slice. The times are simulated.
32 devices in a mesh: dp: 8 (over y, x, core), fsdp: 4 (over z).
Axes of the slice: x: 2, y: 2, z: 4, core: 2. Of those that a mesh axis runs over, the one named last changes fastest.
Arguments:
- tokens: bfloat16 [16384, 768], P(('dp', 'fsdp')), may hold values from -6 to 6
- cotangent: bfloat16 [16384, 768], P(('dp', 'fsdp')), may hold values from -6 to 6
- params: bfloat16 [7087104], P(('dp', 'fsdp'))
- lengths: int32 [64, 2], P(('dp', 'fsdp')), may hold values from 39 to 98, as said below
Outputs:
- block_out: bfloat16 [16384, 768], P(('dp', 'fsdp'))
- input_grad: float32 [16384, 768], P(('dp', 'fsdp'))
- param_grad: float32 [7087104], P(('dp', 'fsdp'))
Inputs may be any that keep to these rules, and one draw needn't show every extreme that they name: `lengths`: row b gives, in order, the visible patches of the 2 images packed from row 0 of buffer b; rows past their sum are padding. Every buffer holds one image of exactly 98 patches.
All inputs are finite; a program needn't handle non-finite values.
Results may differ from a plain program's by a relative error of at most 0.012.
Values may be sent and summed in bfloat16 or wider, within the bound.
A program may use at most 192 MiB of HBM per device.

v0:
```python
import functools
import math

import jax
import jax.numpy as jnp
from jax import lax
from jax.experimental import pallas as pl
from jax.experimental.pallas import tpu as pltpu
from jax.sharding import PartitionSpec as P

AXES = ("dp", "fsdp")
LANES = 128
CORE = 3


class Place:
    def __init__(self, mesh):
        devs = mesh.devices
        spot = lambda d: (*d.coords, d.core_on_chip)
        self.shape = devs.shape
        self.digits = []
        for axis in range(2):
            line = [spot(devs[i, 0] if axis == 0 else devs[0, i]) for i in range(devs.shape[axis])]
            found, stride = [], 1
            while stride < len(line):
                delta = [b - a for a, b in zip(line[0], line[stride])]
                phys = [p for p in range(4) if delta[p]][0]
                step, size = delta[phys], 1
                while (
                    size * stride < len(line)
                    and line[size * stride][phys] - line[0][phys] == size * step
                    and all(line[size * stride][q] == line[0][q] for q in range(4) if q != phys)
                ):
                    size += 1
                found.append((phys, step, size, stride))
                stride *= size
            self.digits.append(found)
        self.size = [1, 1, 1, 1]
        for found in self.digits:
            for phys, _, size, _ in found:
                self.size[phys] *= size
        self.devices = devs.size
        self.chips = math.prod(self.size[:3])
        long = max(range(3), key=lambda p: self.size[p])
        a, b = [p for p in range(3) if p != long]
        self.orders = ((long, a, b), (long, b, a))
        self.shares = (1, 1)
        if self.chips <= 16:
            self.orders += ((a, long, b), (b, long, a))
            self.shares += (2, 2)
        self.classes = len(self.orders)

    def coords(self):
        index = [lax.axis_index(name) for name in AXES]
        out = [0, 0, 0, 0]
        for axis in range(2):
            for phys, step, size, stride in self.digits[axis]:
                out[phys] = out[phys] + ((index[axis] // stride) % size) * step
        return out

    def device(self, coords):
        out = []
        for axis in range(2):
            total = 0
            for phys, step, size, stride in self.digits[axis]:
                total = total + ((coords[phys] // step) % size) * stride
            out.append(total)
        return tuple(out)

    def flat(self, coords):
        dp, fsdp = self.device(coords)
        return dp * self.shape[1] + fsdp

    def chip(self, coords):
        return (coords[0] * self.size[1] + coords[1]) * self.size[2] + coords[2]

    def class_rows(self, rows):
        units = rows // 16
        counts = [units * share // sum(self.shares) for share in self.shares]
        counts[-1] += units - sum(counts)
        out, start = [], 0
        for count in counts:
            out.append((start * 16, count * 16))
            start += count
        return out


def flipped(mine, rel, size):
    total, bit = 0, 1
    while bit < size:
        total = total + bit * (((mine // bit) % 2 + (rel // bit) % 2) % 2)
        bit *= 2
    return total


def both(*conds):
    known = [c for c in conds if isinstance(c, bool)]
    if not all(known):
        return False
    rest = [c for c in conds if not isinstance(c, bool)]
    return functools.reduce(jnp.logical_and, rest) if rest else True


def when(cond, fn):
    if isinstance(cond, bool):
        if cond:
            fn()
    else:
        pl.when(cond)(fn)


def moved(coords, dim, by):
    out = list(coords)
    out[dim] = out[dim] + by
    return out


def partner(coords):
    out = list(coords)
    out[CORE] = 1 - out[CORE]
    return out


def neighbours(place, me):
    out = [(True, partner(me))]
    for dim in range(3):
        if place.size[dim] == 1:
            continue
        if place.size[dim] == 2:
            other = list(me)
            other[dim] = 1 - other[dim]
            out.append((True, other))
        else:
            out.append((me[dim] < place.size[dim] - 1, moved(me, dim, 1)))
            out.append((me[dim] > 0, moved(me, dim, -1)))
    return out


def greet(place, me):
    barrier = pltpu.get_barrier_semaphore()
    nbrs = neighbours(place, me)
    for cond, who in nbrs:
        when(
            cond,
            lambda who=who: pl.semaphore_signal(
                barrier, inc=1, device_id=place.device(who), device_id_type=pl.DeviceIdType.MESH
            ),
        )
    peers = sum(1 if cond is True else jnp.where(cond, 1, 0) for cond, _ in nbrs)
    pl.semaphore_wait(barrier, peers)


def onward(place, order, me, rel, src):
    out = []
    for pos in range(3):
        dim = order[pos]
        size = place.size[dim]
        if size == 1:
            continue
        later = [rel[d] == 0 for d in order[pos + 1 :]]
        if size == 2:
            other = list(me)
            other[dim] = 1 - other[dim]
            out.append((both(*later, rel[dim] == 0), pos, 0, other))
        else:
            for way, by in ((0, 1), (1, -1)):
                if by == 1:
                    here = both(me[dim] >= src[dim], me[dim] < size - 1)
                else:
                    here = both(me[dim] <= src[dim], me[dim] > 0)
                cond = both(*later, here)
                out.append((cond, pos, way, moved(me, dim, by)))
    return out


PASSES = (
    0, 16, 32, 48, 1, 17, 40, 33, 52, 49, 41, 56, 3, 8, 2, 20, 35, 34, 10, 53, 18, 28,
    11, 5, 51, 36, 12, 19, 45, 57, 50, 9, 7, 21, 55, 54, 60, 25, 44, 6, 22, 29, 24, 42,
    58, 27, 37, 26, 59, 43, 15, 23, 4, 39, 61, 14, 30, 13, 62, 38, 63, 31, 47, 46,
)


def walk_parts(place, body, reverse=False, after=None):
    if place.size[:3] == [2, 2, 4]:
        for i, code in enumerate(PASSES[::-1] if reverse else PASSES):
            body(code // 16, ((code // 8) % 2, (code // 4) % 2, code % 4))
            if after is not None:
                after(i)
        return

    def each(rel):
        for k in range(place.classes):
            body(k, rel)

    walk(place, each, reverse)
    if after is not None:
        after(None)


def walk(place, body, reverse=False):
    sizes = place.size[:3]
    if place.chips <= 16:
        rels = [
            (x, y, z) for x in range(sizes[0]) for y in range(sizes[1]) for z in range(sizes[2])
        ]
        rels.sort(key=lambda r: (sum(r), r), reverse=reverse)
        for rel in rels:
            body(rel)
        return

    def step(i, carry):
        i = place.chips - 1 - i if reverse else i
        body((i % sizes[0], (i // sizes[0]) % sizes[1], i // (sizes[0] * sizes[1])))
        return carry

    lax.fori_loop(0, place.chips, step, 0)


def source_of(place, me, rel):
    return [flipped(me[d], rel[d], place.size[d]) for d in range(3)] + [me[CORE]]


def gather_all(place, me, held, send, recv, cross, after=None):
    rows = held.shape[1]
    parts = place.class_rows(rows)

    def copy(k, src, slot, sem, who):
        start, count = parts[k]
        ref = held.at[place.flat(src), pl.ds(start, count), :]
        return pltpu.make_async_remote_copy(
            src_ref=ref,
            dst_ref=ref,
            send_sem=send.at[k, place.chip(src), slot],
            recv_sem=sem.at[k, place.chip(src)],
            device_id=place.device(who),
            device_id_type=pl.DeviceIdType.MESH,
        )

    def sends(k, rel, src, act):
        for cond, pos, way, who in onward(place, place.orders[k], me, rel, src):
            when(cond, lambda: act(copy(k, src, pos * 2 + way, recv, who)))
        act(copy(k, src, 6, cross, partner(me)))

    def go(k, rel):
        src = source_of(place, me, rel)
        home = both(*[r == 0 for r in rel])
        if home is not True:
            away = True if home is False else jnp.logical_not(home)
            when(away, lambda: copy(k, src, 0, recv, me).wait_recv())
        sends(k, rel, src, lambda c: c.start())

    walk_parts(place, go, after=after)

    def drain(rel):
        src = source_of(place, me, rel)
        theirs = partner(src)
        for k in range(place.classes):
            sends(k, rel, src, lambda c: c.wait_send())
            copy(k, theirs, 0, cross, me).wait_recv()

    walk(place, drain)


def gather_sems(place):
    return [
        pltpu.SemaphoreType.DMA((place.classes, place.chips, 7)),
        pltpu.SemaphoreType.DMA((place.classes, place.chips)),
        pltpu.SemaphoreType.DMA((place.classes, place.chips)),
    ]


def slot_plan(place, rows):
    plan = []
    for order in place.orders:
        starts, total = [], 0
        for pos in range(3):
            before = math.prod(place.size[d] for d in order[:pos])
            size = place.size[order[pos]]
            starts.append(total)
            total += before * (1 if size == 2 else size + 1 if size > 1 else 0)
        plan.append((starts, total))
    return plan


def slot_of(place, plan, k, pos, way, at, dest):
    order = place.orders[k]
    index = 0
    for d in order[:pos]:
        index = index * place.size[d] + dest[d]
    dim = order[pos]
    size = place.size[dim]
    if size > 2:
        spot = dest[dim]
        if way == 1:
            spot = spot + jnp.where(at[dim] == dest[dim], size - dest[dim], 0)
        index = index * (size + 1) + spot
    return plan[k][0][pos] + index


def add_rows(dst, a, b, count, step=16):
    def body(i, carry):
        r = pl.ds(pl.multiple_of(i * step, step), step)
        dst(r, a(r).astype(jnp.float32) + b(r).astype(jnp.float32))
        return carry

    lax.fori_loop(0, count // step, body, 0)


def scatter_all(place, me, own, cross, slots, total, sems):
    cross_send, cross_recv, send, recv = sems
    rows = own.shape[1]
    parts = place.class_rows(rows)
    plan = slot_plan(place, rows)

    def swap(dest):
        return pltpu.make_async_remote_copy(
            src_ref=own.at[place.flat(partner(dest))],
            dst_ref=cross.at[place.chip(dest)],
            send_sem=cross_send.at[place.chip(dest)],
            recv_sem=cross_recv.at[place.chip(dest)],
            device_id=place.device(partner(me)),
            device_id_type=pl.DeviceIdType.MESH,
        )

    def pass_on(k, pos, way, dest, to):
        start, count = parts[k]
        slot = slot_of(place, plan, k, pos, way, to, dest)
        return pltpu.make_async_remote_copy(
            src_ref=own.at[place.flat(dest), pl.ds(start, count), :],
            dst_ref=slots[k].at[slot],
            send_sem=send.at[k, place.chip(dest)],
            recv_sem=recv[k].at[slot],
            device_id=place.device(to),
            device_id_type=pl.DeviceIdType.MESH,
        )

    def parents(k, rel, dest):
        order = place.orders[k]
        out = []
        for pos in range(3):
            dim = order[pos]
            size = place.size[dim]
            if size == 1:
                continue
            later = both(*[rel[d] == 0 for d in order[pos + 1 :]])
            if size == 2:
                other = list(me)
                other[dim] = 1 - other[dim]
                away = rel[dim] == 1
                out.append((both(later, away), pos, 0, other))
            else:
                out.append((both(later, me[dim] > dest[dim]), pos, 0, moved(me, dim, -1)))
                out.append((both(later, me[dim] < dest[dim]), pos, 1, moved(me, dim, 1)))
        return out

    walk(place, lambda rel: swap(source_of(place, me, rel)).start(), reverse=True)

    def go(rel):
        dest = source_of(place, me, rel)
        home = both(*[r == 0 for r in rel])
        flat, chip = place.flat(dest), place.chip(dest)
        swap(dest).wait_recv()

        def mix(final):
            for k in range(place.classes):
                start, count = parts[k]

                def rows_of(r):
                    return pl.ds(r.start + start, r.size)

                if final:

                    def put(r, v):
                        total[rows_of(r), :] = v

                    def held(r):
                        return total[rows_of(r), :]

                else:

                    def put(r, v):
                        own[flat, rows_of(r), :] = v.astype(own.dtype)

                    def held(r):
                        return own[flat, rows_of(r), :]

                add_rows(
                    put,
                    lambda r: own[flat, rows_of(r), :],
                    lambda r: cross[chip, rows_of(r), :],
                    count,
                )
                for cond, pos, way, who in onward(place, place.orders[k], me, rel, dest):

                    def take():
                        slot = slot_of(place, plan, k, pos, way, me, dest)
                        pass_on(k, pos, way, dest, me).wait_recv()
                        add_rows(put, held, lambda r: slots[k][slot, r, :], count)

                    when(cond, take)
                if not final:
                    for cond, pos, way, who in parents(k, rel, dest):
                        when(cond, lambda: pass_on(k, pos, way, dest, who).start())

        if isinstance(home, bool):
            mix(home)
        else:
            pl.when(home)(lambda: mix(True))
            pl.when(jnp.logical_not(home))(lambda: mix(False))

    walk(place, go, reverse=True)

    def drain(rel):
        dest = source_of(place, me, rel)
        swap(dest).wait_send()
        for k in range(place.classes):
            for cond, pos, way, who in parents(k, rel, dest):
                when(cond, lambda: pass_on(k, pos, way, dest, who).wait_send())

    walk(place, drain)


def scatter_scratch(place, rows):
    parts = place.class_rows(rows)
    plan = slot_plan(place, rows)
    dma = pltpu.SemaphoreType.DMA
    return (
        [pltpu.VMEM((place.chips, rows, LANES), jnp.bfloat16)],
        [pltpu.VMEM((plan[k][1], parts[k][1], LANES), jnp.bfloat16) for k in range(place.classes)],
        [dma((place.chips,)), dma((place.chips,)), dma((place.classes, place.chips))],
        [dma((plan[k][1],)) for k in range(place.classes)],
    )


D = 768
HEAD_DIM = 64
FF = 3072
EPSILON = 1e-06
NEG_FILL = -1e30
ROOT_HALF = 0.7071067811865476
INV_ROOT_TWO_PI = 0.3989422804014327

PIECES = (
    ("ln1_gain", (D,)),
    ("ln1_bias", (D,)),
    ("w_qkv", (D, 3 * D)),
    ("q_bias", (D,)),
    ("v_bias", (D,)),
    ("w_proj", (D, D)),
    ("proj_bias", (D,)),
    ("ln2_gain", (D,)),
    ("ln2_bias", (D,)),
    ("w_fc1", (D, FF)),
    ("fc1_bias", (FF,)),
    ("w_fc2", (FF, D)),
    ("fc2_bias", (D,)),
)
MATRICES = tuple(name for name, shape in PIECES if len(shape) == 2)
VECTORS = tuple(name for name, shape in PIECES if len(shape) == 1)
SHAPES = dict(PIECES)


def row_bases():
    bases, row = {}, 0
    for name, shape in PIECES:
        bases[name] = row
        row += math.prod(shape) // LANES
    return bases, row


BASES, TOTAL_ROWS = row_bases()
IMAGE_MAX = 98
QKV_BIAS = len(VECTORS)
TABLE = (16, FF)


def part_rows(entries):
    return -(-((LANES - 1 + entries - 1) // LANES + 1) // 16) * 16


def tile(i):
    return pl.ds(pl.multiple_of(i * 16, 16), 16)


def loop(count, body, unroll=1):
    def step(i, carry):
        for u in range(unroll):
            body(i * unroll + u)
        return carry

    whole = count // unroll
    if whole:
        lax.fori_loop(0, whole, step, 0)
    for i in range(whole * unroll, count):
        body(i)


def aligned(raw, held, stage, which, entries):
    rows = held.shape[1]
    shift = (entries * which) % LANES
    stage[0:8, :] = jnp.zeros((8, LANES), jnp.float32)

    def turn(i):
        stage[pl.ds(pl.multiple_of(i * 16 + 8, 8), 16), :] = pltpu.roll(
            raw[tile(i), :].astype(jnp.float32), shift, 1
        )

    loop(rows // 16, turn, 8)

    def merge(i):
        lane = lax.broadcasted_iota(jnp.int32, (16, LANES), 1)
        now = stage[pl.ds(i * 16 + 8, 16), :]
        before = stage[pl.ds(i * 16 + 7, 16), :]
        held[which, tile(i), :] = jnp.where(lane < shift, before, now).astype(held.dtype)

    loop(rows // 16, merge, 8)


def round_up(value, unit):
    return -(-value // unit) * unit


class Span:
    def __init__(self, low, high, name, first, depth, vectors):
        self.low, self.high = low, high
        self.name, self.first, self.depth = name, first, depth
        self.vectors = vectors


def spans(cuts):
    out, row, early = [], 0, []
    for name, shape in PIECES:
        count = math.prod(shape) // LANES
        if len(shape) == 1:
            if out:
                out[-1].vectors.append(name)
                out[-1].high = row + count
            else:
                early.append(name)
        else:
            depth = shape[0] // cuts[name]
            blocks = shape[1] // LANES
            for c in range(cuts[name]):
                start = row + c * depth * blocks
                span = Span(start, start + depth * blocks, name, c * depth, depth, [])
                if not out:
                    span.low, span.vectors = 0, early
                out.append(span)
        row += count
    return out


GATHER_SPANS = spans({name: 1 for name in MATRICES})
SCATTER_SPANS = spans({"w_qkv": 2, "w_proj": 1, "w_fc1": 2, "w_fc2": 2})


def stage_rows(spans_, rows):
    return round_up(max(s.high - s.low for s in spans_), 16) + 2 * rows + 32


def owners(span, entries):
    return (span.low * LANES) // entries, (span.high * LANES - 1) // entries


def spread(held, stage, span, entries):
    rows = held.shape[1]
    low, high = owners(span, entries)

    def one(i):
        d = low + i
        base = (entries * d) // LANES - span.low + rows
        cut = (entries * d) % LANES
        first = stage[pl.ds(base, 1), :]

        def body(t):
            stage[pl.ds(base + t * 16, 16), :] = held[d, tile(t), :].astype(jnp.float32)

        loop(rows // 16, body, 8)
        row = stage[pl.ds(base, 1), :]
        stage[pl.ds(base, 1), :] = jnp.where(cut != 0, row + first, row)

    loop(high - low + 1, one)


def form(stage, span, margin, out):
    blocks = SHAPES[span.name][1] // LANES
    base = margin + BASES[span.name] + span.first * blocks - span.low

    def body(i):
        for j in range(blocks):
            out[tile(i + span.first // 16), j * LANES : (j + 1) * LANES] = stage[
                pl.ds(base + i * 16 * blocks + j, 16, stride=blocks), :
            ].astype(out.dtype)

    loop(span.depth // 16, body, max(1, 24 // blocks))


def vector_rows(stage, span, margin, table):
    for name in span.vectors:
        at = margin + BASES[name] - span.low
        row = VECTORS.index(name)
        for j in range(SHAPES[name][0] // LANES):
            table[row : row + 1, j * LANES : (j + 1) * LANES] = stage[at + j : at + j + 1, :]


def vector(table, name):
    row = VECTORS.index(name)
    return table[row : row + 1, 0 : SHAPES[name][0]]


def lay(stage, span, margin, first, value):
    blocks = SHAPES[span.name][1] // LANES
    base = margin + BASES[span.name] - span.low + first * blocks
    for i in range(value.shape[0] // 16):
        for j in range(blocks):
            stage[pl.ds(base + i * 16 * blocks + j, 16, stride=blocks), :] = value[
                i * 16 : (i + 1) * 16, j * LANES : (j + 1) * LANES
            ]


def lay_vectors(stage, span, margin, table):
    for name in span.vectors:
        at = margin + BASES[name] - span.low
        row = VECTORS.index(name)
        for j in range(SHAPES[name][0] // LANES):
            stage[at + j : at + j + 1, :] = table[row : row + 1, j * LANES : (j + 1) * LANES]


def cut(stage, span, own, entries):
    rows = own.shape[1]
    low, high = owners(span, entries)

    def whole(d):
        base = (entries * d) // LANES - span.low + rows

        def body(t):
            own[d, tile(t), :] = stage[pl.ds(base + t * 16, 16), :].astype(own.dtype)

        loop(rows // 16, body, 8)

    def edge(d):
        base = (entries * d) // LANES - span.low + rows

        def body(t):
            now = stage[pl.ds(base + t * 16, 16), :]
            row = base + t * 16 - rows + lax.broadcasted_iota(jnp.int32, (16, LANES), 0)
            inside = jnp.logical_and(row >= 0, row < span.high - span.low)
            before = own[d, tile(t), :].astype(jnp.float32)
            own[d, tile(t), :] = jnp.where(inside, now, before).astype(own.dtype)

        loop(rows // 16, body, 8)

    edge(low)
    if high - low > 1:
        loop(high - low - 1, lambda i: whole(low + 1 + i))
    if high > low:
        edge(high)


def mean_of(v):
    return jnp.sum(v, axis=-1, keepdims=True) * (1.0 / v.shape[-1])


def normalize(v):
    centred = v - mean_of(v)
    inv_std = lax.rsqrt(mean_of(centred * centred) + EPSILON)
    return centred * inv_std, inv_std


def norm_back(grad_out, normed, inv_std, gain):
    grad_norm = grad_out * gain
    return inv_std * (grad_norm - mean_of(grad_norm) - normed * mean_of(grad_norm * normed))


def dot(a, b, left=1, right=0):
    return lax.dot_general(
        a, b, (((left,), (right,)), ((), ())), preferred_element_type=jnp.float32
    )


def columns(width, block, body):
    loop(width // block, lambda i: body(pl.ds(pl.multiple_of(i * block, block), block)))


def segments(lengths, b, images, shape, dim):
    position = lax.broadcasted_iota(jnp.int32, shape, dim)
    total, seg = 0, jnp.zeros(shape, jnp.int32)
    for i in range(images):
        total = total + lengths[b, i]
        seg = seg + jnp.where(position >= total, 1, 0)
    return seg


def valid_rows(lengths, b, images, count):
    return jnp.where(segments(lengths, b, images, (count, 1), 0) < images, 1.0, 0.0)


class Sizes:
    def __init__(self, tokens, lengths):
        self.buffers, self.images = lengths.shape
        self.full = tokens.shape[0] // self.buffers
        self.rows = min(self.full, round_up(self.images * IMAGE_MAX, 16))
        self.total = self.rows * self.buffers
        self.pairs = D // LANES

    def at(self, b):
        return slice(b * self.rows, (b + 1) * self.rows)

    def given(self, b):
        return slice(b * self.full, b * self.full + self.rows)


def low(v):
    return v.astype(jnp.bfloat16)


def half_lanes(rows):
    lane = lax.broadcasted_iota(jnp.int32, (rows, LANES), 1)
    first = low(jnp.where(lane < HEAD_DIM, 1.0, 0.0))
    return first, low(jnp.where(lane < HEAD_DIM, 0.0, 1.0))


SCALE = 1.0 / math.sqrt(HEAD_DIM)
SAVED = ("attn_in", "qkv", "probs", "mix", "mid", "mlp_in", "act", "slope")


def saved_shapes(sz):
    t = sz.total
    bf = jnp.bfloat16
    return {
        "attn_in": ((t, D), bf),
        "qkv": ((t, 3 * D), bf),
        "probs": ((sz.buffers * sz.pairs * 2, sz.rows, sz.rows), bf),
        "mix": ((t, D), bf),
        "mid": ((t, D), jnp.float32),
        "mlp_in": ((t, D), bf),
        "act": ((t, FF), bf),
        "slope": ((t, FF), bf),
    }


def forward_kernel(place, entries, sz, raw, tokens, lengths, *refs):
    mats, refs = dict(zip(MATRICES, refs[:4])), refs[4:]
    out_saved, refs = dict(zip(SAVED, refs[:8])), refs[8:]
    table, block_out, refs = refs[0], refs[1], refs[2:]
    held, stage, refs = refs[0], refs[1], refs[2:]
    w, refs = dict(zip(MATRICES, refs[:4])), refs[4:]
    a, refs = dict(zip(SAVED, refs[:8])), refs[8:]
    normed = refs[0]
    send, recv, cross, done_w, done_a = refs[1:]
    me = place.coords()
    margin = held.shape[1]

    aligned(raw, held, stage, place.flat(me), entries)
    greet(place, me)

    def norm_first(i):
        for b in range(sz.buffers):
            x = tokens[pl.ds(pl.multiple_of(b * sz.full + i * 16, 16), 16), :].astype(jnp.float32)
            normed[pl.ds(pl.multiple_of(b * sz.rows + i * 16, 16), 16), :] = normalize(x)[0]

    def after(i):
        if i is None or i == 8:
            loop(sz.rows // 16, norm_first)

    gather_all(place, me, held, send, recv, cross, after)

    def keep(name):
        pltpu.make_async_copy(a[name], out_saved[name], done_a.at[SAVED.index(name)]).start()

    for span in GATHER_SPANS:
        name = span.name
        spread(held, stage, span, entries)
        form(stage, span, margin, w[name])
        vector_rows(stage, span, margin, table)
        m = MATRICES.index(name)
        pltpu.make_async_copy(w[name], mats[name], done_w.at[m]).start()
    table[QKV_BIAS : QKV_BIAS + 1, 0:D] = vector(table, "q_bias")
    table[QKV_BIAS : QKV_BIAS + 1, D : 2 * D] = jnp.zeros((1, D), jnp.float32)
    table[QKV_BIAS : QKV_BIAS + 1, 2 * D : 3 * D] = vector(table, "v_bias")

    def scale_first(i):
        a["attn_in"][tile(i), :] = low(
            normed[tile(i), :] * vector(table, "ln1_gain") + vector(table, "ln1_bias")
        )

    loop(sz.total // 16, scale_first)
    keep("attn_in")

    def to_qkv(c):
        a["qkv"][:, c] = low(
            dot(a["attn_in"][...], w["w_qkv"][:, c]) + table[QKV_BIAS : QKV_BIAS + 1, c]
        )

    columns(3 * D, 256, to_qkv)
    keep("qkv")

    qkv, probs, mix = a["qkv"], a["probs"], a["mix"]
    for b in range(sz.buffers):
        rows = sz.at(b)
        seg_r = segments(lengths, b, sz.images, (sz.rows, 1), 0)
        seg_c = segments(lengths, b, sz.images, (1, sz.rows), 1)

        def attend(p):
            halves = half_lanes(sz.rows)
            at = lambda part: pl.ds(pl.multiple_of(part * D + p * LANES, LANES), LANES)
            q, k, v = (qkv[rows, at(part)] for part in range(3))
            mixed = None
            for h in range(2):
                s = dot(q * (halves[h] * SCALE).astype(q.dtype), k, 1, 1)
                s = jnp.where(seg_r == seg_c, s, NEG_FILL)
                e = jnp.exp(s - jnp.max(s, axis=-1, keepdims=True))
                pr = low(e * (1.0 / jnp.sum(e, axis=-1, keepdims=True)))
                probs[(b * sz.pairs + p) * 2 + h] = pr
                part = dot(pr, v * halves[h])
                mixed = part if mixed is None else mixed + part
            mix[rows, at(0)] = low(mixed)

        loop(sz.pairs, attend)
    keep("probs")
    keep("mix")

    def to_mid(c):
        made = dot(mix[...], w["w_proj"][:, c]) + table[
            VECTORS.index("proj_bias") : VECTORS.index("proj_bias") + 1, c
        ]
        for b in range(sz.buffers):
            a["mid"][sz.at(b), c] = (
                tokens[sz.given(b), c].astype(jnp.float32) + made[sz.at(b), :]
            )

    columns(D, 256, to_mid)
    keep("mid")

    def norm_second(i):
        a["mlp_in"][tile(i), :] = low(
            normalize(a["mid"][tile(i), :])[0] * vector(table, "ln2_gain")
            + vector(table, "ln2_bias")
        )

    loop(sz.total // 16, norm_second)
    keep("mlp_in")

    def to_act(c):
        at = VECTORS.index("fc1_bias")
        pre = dot(a["mlp_in"][...], w["w_fc1"][:, c]) + table[at : at + 1, c]
        phi = 0.5 * (1.0 + lax.erf(pre * ROOT_HALF))
        a["act"][:, c] = low(pre * phi)
        a["slope"][:, c] = low(phi + pre * jnp.exp(-0.5 * pre * pre) * INV_ROOT_TWO_PI)

    columns(FF, 256, to_act)
    keep("act")
    keep("slope")

    def to_out(c):
        at = VECTORS.index("fc2_bias")
        made = dot(a["act"][...], w["w_fc2"][:, c]) + table[at : at + 1, c]
        for b in range(sz.buffers):
            valid = valid_rows(lengths, b, sz.images, sz.rows)
            block_out[sz.given(b), c] = low(valid * (a["mid"][sz.at(b), c] + made[sz.at(b), :]))
            if sz.full > sz.rows:
                block_out[b * sz.full + sz.rows : (b + 1) * sz.full, c] = jnp.zeros(
                    (sz.full - sz.rows, made.shape[1]), jnp.bfloat16
                )

    columns(D, 256, to_out)
    for m, name in enumerate(MATRICES):
        pltpu.make_async_copy(w[name], mats[name], done_w.at[m]).wait()
    for i, name in enumerate(SAVED):
        pltpu.make_async_copy(a[name], out_saved[name], done_a.at[i]).wait()


def forward(place, tokens, params, lengths):
    entries = params.shape[0]
    rows = part_rows(entries)
    sz = Sizes(tokens, lengths)
    raw = jnp.pad(params, (0, rows * LANES - entries)).reshape(rows, LANES)
    any_spec = pl.BlockSpec(memory_space=pl.ANY)
    vmem = pl.BlockSpec(memory_space=pltpu.VMEM)
    smem = pl.BlockSpec(memory_space=pltpu.SMEM)
    saved = saved_shapes(sz)
    bf = jnp.bfloat16
    outs = pl.pallas_call(
        functools.partial(forward_kernel, place, entries, sz),
        out_shape=[jax.ShapeDtypeStruct(SHAPES[n], bf) for n in MATRICES]
        + [jax.ShapeDtypeStruct(*saved[n]) for n in SAVED]
        + [jax.ShapeDtypeStruct(TABLE, jnp.float32), jax.ShapeDtypeStruct(tokens.shape, bf)],
        in_specs=[vmem, vmem, smem],
        out_specs=[any_spec] * 12 + [vmem, vmem],
        scratch_shapes=[
            pltpu.VMEM((place.devices, rows, LANES), bf),
            pltpu.VMEM((stage_rows(GATHER_SPANS, rows), LANES), jnp.float32),
        ]
        + [pltpu.VMEM(SHAPES[n], bf) for n in MATRICES]
        + [pltpu.VMEM(*saved[n]) for n in SAVED]
        + [pltpu.VMEM((sz.total, D), jnp.float32)]
        + gather_sems(place)
        + [pltpu.SemaphoreType.DMA((4,)), pltpu.SemaphoreType.DMA((8,))],
        compiler_params=pltpu.CompilerParams(
            collective_id=0, has_side_effects=True, vmem_limit_bytes=67 * 10**6
        ),
        name="forward",
    )(raw, tokens, lengths)
    return dict(zip(MATRICES, outs[:4])), dict(zip(SAVED, outs[4:12])), outs[12], outs[13]


SUMS = tuple(VECTORS)


def backward_kernel(place, entries, sz, tokens, cotangent, lengths, table, *refs):
    mats, refs = dict(zip(MATRICES, refs[:4])), refs[4:]
    given, refs = dict(zip(SAVED, refs[:8])), refs[8:]
    out, input_grad, refs = refs[0], refs[1], refs[2:]
    own, cross, refs = refs[0], refs[1], refs[2:]
    n = place.classes
    slots, refs = refs[:n], refs[n:]
    cross_send, cross_recv, send = refs[:3]
    recv, refs = refs[3 : 3 + n], refs[3 + n :]
    stage, total, sums, refs = refs[0], refs[1], refs[2], refs[3:]
    big_a, big_b, refs = refs[0], refs[1], refs[2:]
    wide, slope, qkv, probs, mix, mid, narrow, x, g, temp, blank, load, done = refs
    me = place.coords()
    margin = own.shape[1]
    count = sz.total
    order = ("g", "act", "w_fc2", "slope", "mlp_in", "w_fc1", "mid", "mix", "x", "qkv", "probs")

    def fetches(name):
        sem = load.at[order.index(name)]
        if name in ("g", "x"):
            src, dst = (cotangent, g) if name == "g" else (tokens, x)
            return [
                pltpu.make_async_copy(
                    src.at[sz.given(b)],
                    dst.at[sz.at(b)],
                    load.at[order.index(name) if b == 0 else len(order) + 10 + 2 * b + (name == "g")],
                )
                for b in range(sz.buffers)
            ]
        return [pltpu.make_async_copy(*places[name], sem)]

    places = {
        "act": (given["act"], wide),
        "slope": (given["slope"], slope),
        "mlp_in": (given["mlp_in"], narrow),
        "mid": (given["mid"], mid),
        "mix": (given["mix"], mix),
        "qkv": (given["qkv"], qkv),
        "probs": (given["probs"], probs),
        "w_fc2": (mats["w_fc2"], big_a),
        "w_fc1": (mats["w_fc1"], big_b),
    }

    def begin(name):
        for c in fetches(name):
            c.start()

    def ready(name):
        for c in fetches(name):
            c.wait()

    for name in order:
        begin(name)
    greet(place, me)

    def sum_to(name, c, value):
        at = SUMS.index(name)
        sums[at : at + 1, c] = value

    def ones():
        return jnp.ones((8, count), jnp.bfloat16)

    def column_sums(name, ref, width):
        def body(c):
            sum_to(name, c, dot(ones(), ref[:, c])[0:1, :])

        columns(width, 256, body)

    def pieces(name, left, right, block):
        for span in [s for s in SCATTER_SPANS if s.name == name]:

            def body(i):
                first = pl.multiple_of(span.first + i * block, block)
                lay(stage, span, margin, first, dot(left[:, pl.ds(first, block)], right(), 0, 0))

            loop(span.depth // block, body)
            yield span

    def finish(span):
        lay_vectors(stage, span, margin, sums)
        cut(stage, span, own, entries)

    ready("g")
    for b in range(sz.buffers):
        rows = sz.at(b)
        valid = valid_rows(lengths, b, sz.images, sz.rows)
        g[rows, :] = low(g[rows, :].astype(jnp.float32) * valid)
    ready("act")
    column_sums("fc2_bias", g, D)
    for span in pieces("w_fc2", wide, lambda: g[...], 256):
        finish(span)

    ready("w_fc2")
    ready("slope")

    def to_pre(i):
        c = pl.ds(pl.multiple_of(i * 256, 256), 256)
        made = dot(g[...], big_a[c, :], 1, 1)
        wide[:, c] = low(made * slope[:, c].astype(jnp.float32))

    loop(FF // 256, to_pre)
    late = [
        pltpu.make_async_copy(
            mats["w_qkv"].at[:, i * D : (i + 1) * D],
            big_a.at[i * D : (i + 1) * D],
            load.at[len(order) + 8 + i],
        )
        for i in range(3)
    ]
    late.append(
        pltpu.make_async_copy(mats["w_proj"], big_a.at[3 * D : 4 * D], load.at[len(order) + 11])
    )
    for c in reversed(late):
        c.start()
    ready("mlp_in")
    column_sums("fc1_bias", wide, FF)
    for span in pieces("w_fc1", narrow, lambda: wide[...], 128):
        finish(span)

    attn_load = pltpu.make_async_copy(given["attn_in"], narrow, load.at[len(order) + 7])
    attn_load.start()
    ready("w_fc1")

    def to_mlp(i):
        c = pl.ds(pl.multiple_of(i * 256, 256), 256)
        temp[:, c] = dot(wide[...], big_b[c, :], 1, 1)

    loop(D // 256, to_mlp)
    ready("mid")

    def column_add(name, value, first):
        at = SUMS.index(name)
        part = jnp.sum(value, axis=0, keepdims=True)
        before = sums[at : at + 1, 0:D]
        sums[at : at + 1, 0:D] = part if first else before + part

    def clear(name):
        at = SUMS.index(name)
        sums[at : at + 1, 0:D] = jnp.zeros((1, D), jnp.float32)

    clear("ln2_gain")
    clear("ln2_bias")

    def back_second(i):
        normed, inv = normalize(mid[tile(i), :])
        d = temp[tile(i), :]
        column_add("ln2_gain", d * normed, False)
        column_add("ln2_bias", d, False)
        v = g[tile(i), :].astype(jnp.float32) + norm_back(d, normed, inv, vector(table, "ln2_gain"))
        mid[tile(i), :] = v
        g[tile(i), :] = low(v)

    loop(count // 16, back_second)
    ready("mix")
    column_sums("proj_bias", g, D)
    for span in pieces("w_proj", mix, lambda: g[...], 256):
        finish(span)
    late[3].wait()

    def to_mix(i):
        c = pl.ds(pl.multiple_of(i * 256, 256), 256)
        rows = pl.ds(pl.multiple_of(3 * D + i * 256, 256), 256)
        slope[:, c] = low(dot(g[...], big_a[rows, :], 1, 1))

    loop(D // 256, to_mix)
    ready("qkv")
    ready("probs")
    for b in range(sz.buffers):
        rows = sz.at(b)

        def attend(p):
            halves = half_lanes(sz.rows)
            at = lambda part: pl.ds(pl.multiple_of(part * D + p * LANES, LANES), LANES)
            q, k, v = (qkv[rows, at(part)] for part in range(3))
            dm = slope[rows, at(0)]
            dq = dk = dv = 0.0
            for h in range(2):
                pr = probs[(b * sz.pairs + p) * 2 + h]
                dmh = dm * halves[h]
                dp = dot(dmh, v, 1, 1)
                prf = pr.astype(jnp.float32)
                ds = low(prf * (dp - jnp.sum(prf * dp, axis=-1, keepdims=True)))
                dv = dv + dot(pr, dmh, 0, 0)
                dq = dq + dot(ds, k * halves[h])
                dk = dk + dot(ds, q * halves[h], 0, 0)
            wide[rows, at(0)] = low(dq * SCALE)
            wide[rows, at(1)] = low(dk * SCALE)
            wide[rows, at(2)] = low(dv)

        loop(sz.pairs, attend)
    for c in late[:3]:
        c.wait()

    def to_attn(i):
        c = pl.ds(pl.multiple_of(i * 256, 256), 256)
        made = None
        for part in range(3):
            rows = pl.ds(pl.multiple_of(part * D + i * 256, 256), 256)
            term = dot(wide[:, part * D : (part + 1) * D], big_a[rows, :], 1, 1)
            made = term if made is None else made + term
        temp[:, c] = made

    loop(D // 256, to_attn)
    ready("x")
    clear("ln1_gain")
    clear("ln1_bias")

    def back_first(i):
        normed, inv = normalize(x[tile(i), :].astype(jnp.float32))
        d = temp[tile(i), :]
        column_add("ln1_gain", d * normed, False)
        column_add("ln1_bias", d, False)
        mid[tile(i), :] = mid[tile(i), :] + norm_back(d, normed, inv, vector(table, "ln1_gain"))

    loop(count // 16, back_first)
    outs = []
    for b in range(sz.buffers):
        outs.append(
            pltpu.make_async_copy(mid.at[sz.at(b)], input_grad.at[sz.given(b)], done.at[2 * b])
        )
        if sz.full > sz.rows:
            blank[...] = jnp.zeros(blank.shape, blank.dtype)
            outs.append(
                pltpu.make_async_copy(
                    blank,
                    input_grad.at[b * sz.full + sz.rows : (b + 1) * sz.full],
                    done.at[2 * b + 1],
                )
            )
    for c in outs:
        c.start()

    attn_load.wait()

    def qv_sums(c):
        wide_sum = dot(ones(), wide[:, c])[0:1, :]
        sums[len(SUMS) : len(SUMS) + 1, c] = wide_sum

    columns(3 * D, 256, qv_sums)
    for name, part in (("q_bias", 0), ("v_bias", 2)):
        at = SUMS.index(name)
        sums[at : at + 1, 0:D] = sums[len(SUMS) : len(SUMS) + 1, part * D : (part + 1) * D]
    for span in pieces("w_qkv", narrow, lambda: wide[:, 0 : 3 * D], 128):
        finish(span)

    scatter_all(place, me, own, cross, slots, total, (cross_send, cross_recv, send, recv))
    shift = (entries * place.flat(me)) % LANES
    back = (LANES - shift) % LANES
    rows = own.shape[1]

    def turn(i):
        total[tile(i), :] = pltpu.roll(total[tile(i), :], back, 1)

    loop(rows // 16, turn, 8)

    def merge(i):
        lane = lax.broadcasted_iota(jnp.int32, (16, LANES), 1)
        now = total[pl.ds(i * 16, 16), :]
        after = total[pl.ds(i * 16 + 1, 16), :]
        out[tile(i), :] = jnp.where(lane < LANES - shift, now, after)

    loop(rows // 16, merge, 8)
    for c in outs:
        c.wait()


def backward(place, tokens, cotangent, lengths, mats, saved, table, entries):
    rows = part_rows(entries)
    sz = Sizes(tokens, lengths)
    cross, slots, sems, recv = scatter_scratch(place, rows)
    any_spec = pl.BlockSpec(memory_space=pl.ANY)
    vmem = pl.BlockSpec(memory_space=pltpu.VMEM)
    smem = pl.BlockSpec(memory_space=pltpu.SMEM)
    bf, f32 = jnp.bfloat16, jnp.float32
    shapes = saved_shapes(sz)
    scratch = lambda name: pltpu.VMEM(*shapes[name])
    out, input_grad = pl.pallas_call(
        functools.partial(backward_kernel, place, entries, sz),
        out_shape=[
            jax.ShapeDtypeStruct((rows, LANES), f32),
            jax.ShapeDtypeStruct(tokens.shape, f32),
        ],
        in_specs=[any_spec, any_spec, smem, vmem] + [any_spec] * 12,
        out_specs=[vmem, any_spec],
        scratch_shapes=[pltpu.VMEM((place.devices, rows, LANES), bf)]
        + cross
        + slots
        + sems
        + recv
        + [
            pltpu.VMEM((stage_rows(SCATTER_SPANS, rows), LANES), f32),
            pltpu.VMEM((rows + 16, LANES), f32),
            pltpu.VMEM(TABLE, f32),
            pltpu.VMEM((FF, D), bf),
            pltpu.VMEM((D, FF), bf),
            scratch("act"),
            scratch("slope"),
            scratch("qkv"),
            scratch("probs"),
            scratch("mix"),
            scratch("mid"),
            scratch("mlp_in"),
            pltpu.VMEM((sz.total, D), bf),
            pltpu.VMEM((sz.total, D), bf),
            pltpu.VMEM((sz.total, D), f32),
            pltpu.VMEM((max(8, sz.full - sz.rows), D), f32),
            pltpu.SemaphoreType.DMA((24 + 2 * sz.buffers,)),
            pltpu.SemaphoreType.DMA((2 * sz.buffers,)),
        ],
        compiler_params=pltpu.CompilerParams(
            collective_id=1, has_side_effects=True, vmem_limit_bytes=67 * 10**6
        ),
        name="backward",
    )(tokens, cotangent, lengths, table, *[mats[m] for m in MATRICES], *[saved[s] for s in SAVED])
    return input_grad, out.reshape(-1)[:entries]


def solution(mesh):
    place = Place(mesh)

    def shards(tokens, cotangent, params, lengths):
        mats, saved, table, out = forward(place, tokens, params, lengths)
        input_grad, grad = backward(
            place, tokens, cotangent, lengths, mats, saved, table, params.shape[0]
        )
        return out, input_grad, grad

    rows, flat = P(AXES, None), P(AXES)
    return jax.shard_map(
        shards,
        mesh=mesh,
        in_specs=(rows, rows, flat, rows),
        out_specs=(rows, rows, flat),
        check_vma=False,
    )
```

profile of v0, /device:TPU:0, one launch (start us, length us, event | category | flops | bytes accessed | tf_op | source)
XLA Modules:
  0.0 261.6 jit_solution(2427143022253388117)
XLA Ops:
  0.6 1.8 pad_bitcast_fusion.raw
  2.4 109.0 %forward.1 = (bf16[768,2304]{1,0:T(8,128)(2,1)}, bf16[768,768]{1,0:T(8,128)(2,1)}, bf16[768,3072]{1,0:T(8,128)(2,1)}, bf16[3072,768]{1,0:T(8,128)(2,1)}, bf16[41...) custom-call(bf16[1744,128]{1,0:T(8,128)(2,1)} %pad_bitcast_fusion.ra, ...), custom_call_target="tpu_custom_call" | custom-call | tf_op jit(solution)/shard_map/forward/pallas_call | solution.py:883
  111.5 144.7 %backward.1 = (f32[1744,128]{1,0:T(8,128)}, f32[512,768]{1,0:T(8,128)}) custom-call(bf16[512,768]{1,0:T(8,128)(2,1)} %tokens.3, bf16[512,768]{1,0:T(8,128)(2,1)} %cotangent.1, s32[2,2]{1,0:T(2,128)} %lengths.3, f32[16,3072]{1,0:T(8,128)} %get-tuple-element.20.table, bf16[768,2304]{1,0:T(8,128)(2,1)} %get-tuple-element.21.refs_0_, ...), custom_call_target="tpu_custom_call" | custom-call | tf_op jit(solution)/shard_map/backward/pallas_call | solution.py:1186
  256.1 0.0 copy-start
  256.1 2.3 slice.4
  258.4 2.1 copy.9
  260.5 0.0 copy-done
  260.5 1.1 copy.10
Async XLA Ops:
  256.1 4.3 %copy-start = (f32[512,768]{1,0:T(8,128)S(1)}, f32[512,768]{1,0:T(8,128)}, u32[]{:S(2)}) copy-start(f32[512,768]{1,0:T(8,128)} %get-tuple-element.39) | copy-start | bytes 4718596
where the time goes:
time: 262 us
  Pallas kernels  254 us (97%)
  local copies, waits for them, and re-layouts  7.28 us (3%)
    pallas_call x1, Pallas kernels, backward(): pl.pallas_call(functools.partial(backward_kernel, place, entries, sz), ou...  145 us
    pallas_call x1, Pallas kernels, forward(): pl.pallas_call(functools.partial(forward_kernel, place, entries, sz), out...  109 us

commit v1 on v0

--- a/solution.py
+++ b/solution.py
@@ -297,13 +297,15 @@
     return plan[k][0][pos] + index
 
 
-def add_rows(dst, a, b, count, step=16):
-    def body(i, carry):
-        r = pl.ds(pl.multiple_of(i * step, step), step)
-        dst(r, a(r).astype(jnp.float32) + b(r).astype(jnp.float32))
-        return carry
-
-    lax.fori_loop(0, count // step, body, 0)
+def add_rows(dst, terms, count):
+    def body(i):
+        r = tile(i)
+        value = terms[0](r).astype(jnp.float32)
+        for term in terms[1:]:
+            value = value + term(r).astype(jnp.float32)
+        dst(r, value)
+
+    loop(count // 16, body, 4)
 
 
 def scatter_all(place, me, own, cross, slots, total, sems):
@@ -355,52 +357,57 @@
 
     walk(place, lambda rel: swap(source_of(place, me, rel)).start(), reverse=True)
 
-    def go(rel):
+    swapped = set()
+
+    def go(k, rel):
         dest = source_of(place, me, rel)
         home = both(*[r == 0 for r in rel])
         flat, chip = place.flat(dest), place.chip(dest)
-        swap(dest).wait_recv()
+        if isinstance(home, bool):
+            if rel not in swapped:
+                swap(dest).wait_recv()
+            swapped.add(rel)
+        elif k == 0:
+            swap(dest).wait_recv()
 
         def mix(final):
-            for k in range(place.classes):
-                start, count = parts[k]
-
-                def rows_of(r):
-                    return pl.ds(r.start + start, r.size)
-
-                if final:
-
-                    def put(r, v):
-                        total[rows_of(r), :] = v
-
-                    def held(r):
-                        return total[rows_of(r), :]
-
-                else:
-
-                    def put(r, v):
-                        own[flat, rows_of(r), :] = v.astype(own.dtype)
-
-                    def held(r):
-                        return own[flat, rows_of(r), :]
-
-                add_rows(
-                    put,
-                    lambda r: own[flat, rows_of(r), :],
-                    lambda r: cross[chip, rows_of(r), :],
-                    count,
-                )
-                for cond, pos, way, who in onward(place, place.orders[k], me, rel, dest):
-
-                    def take():
-                        slot = slot_of(place, plan, k, pos, way, me, dest)
-                        pass_on(k, pos, way, dest, me).wait_recv()
-                        add_rows(put, held, lambda r: slots[k][slot, r, :], count)
-
-                    when(cond, take)
-                if not final:
-                    for cond, pos, way, who in parents(k, rel, dest):
-                        when(cond, lambda: pass_on(k, pos, way, dest, who).start())
+            start, count = parts[k]
+
+            def rows_of(r):
+                return pl.ds(r.start + start, r.size)
+
+            if final:
+
+                def put(r, v):
+                    total[rows_of(r), :] = v
+
+                def held(r):
+                    return total[rows_of(r), :]
+
+            else:
+
+                def put(r, v):
+                    own[flat, rows_of(r), :] = v.astype(own.dtype)
+
+                def held(r):
+                    return own[flat, rows_of(r), :]
+
+            def kid(pos, way):
+                slot = slot_of(place, plan, k, pos, way, me, dest)
+                pass_on(k, pos, way, dest, me).wait_recv()
+                return lambda r: slots[k][slot, r, :]
+
+            kids = onward(place, place.orders[k], me, rel, dest)
+            terms = [lambda r: own[flat, rows_of(r), :], lambda r: cross[chip, rows_of(r), :]]
+            terms += [kid(pos, way) for cond, pos, way, _ in kids if cond is True]
+            add_rows(put, terms, count)
+            for cond, pos, way, _ in kids:
+                if isinstance(cond, bool):
+                    continue
+                pl.when(cond)(lambda: add_rows(put, [held, kid(pos, way)], count))
+            if not final:
+                for cond, pos, way, who in parents(k, rel, dest):
+                    when(cond, lambda: pass_on(k, pos, way, dest, who).start())
 
         if isinstance(home, bool):
             mix(home)
@@ -408,7 +415,7 @@
             pl.when(home)(lambda: mix(True))
             pl.when(jnp.logical_not(home))(lambda: mix(False))
 
-    walk(place, go, reverse=True)
+    walk_parts(place, go, reverse=True)
 
     def drain(rel):
         dest = source_of(place, me, rel)
@@ -918,7 +925,7 @@
     recv, refs = refs[3 : 3 + n], refs[3 + n :]
     stage, total, sums, refs = refs[0], refs[1], refs[2], refs[3:]
     big_a, big_b, refs = refs[0], refs[1], refs[2:]
-    wide, slope, qkv, probs, mix, mid, narrow, x, g, temp, blank, load, done = refs
+    wide, slope, qkv, probs, mix, mid, narrow, x, g, temp, blank, partial, load, done = refs
     me = place.coords()
     margin = own.shape[1]
     count = sz.total
@@ -1037,29 +1044,30 @@
     loop(D // 256, to_mlp)
     ready("mid")
 
-    def column_add(name, value, first):
-        at = SUMS.index(name)
-        part = jnp.sum(value, axis=0, keepdims=True)
-        before = sums[at : at + 1, 0:D]
-        sums[at : at + 1, 0:D] = part if first else before + part
-
-    def clear(name):
-        at = SUMS.index(name)
-        sums[at : at + 1, 0:D] = jnp.zeros((1, D), jnp.float32)
-
-    clear("ln2_gain")
-    clear("ln2_bias")
+    def folded(v):
+        return v[0:8, :] + v[8:16, :]
+
+    def norm_sums(body, gain, bias):
+        partial[...] = jnp.zeros(partial.shape, jnp.float32)
+
+        def step(i):
+            for which, value in enumerate(body(i)):
+                partial[which] += folded(value)
+
+        loop(count // 16, step, 2)
+        for which, name in enumerate((gain, bias)):
+            at = SUMS.index(name)
+            sums[at : at + 1, 0:D] = jnp.sum(partial[which], axis=0, keepdims=True)
 
     def back_second(i):
         normed, inv = normalize(mid[tile(i), :])
         d = temp[tile(i), :]
-        column_add("ln2_gain", d * normed, False)
-        column_add("ln2_bias", d, False)
         v = g[tile(i), :].astype(jnp.float32) + norm_back(d, normed, inv, vector(table, "ln2_gain"))
         mid[tile(i), :] = v
         g[tile(i), :] = low(v)
-
-    loop(count // 16, back_second)
+        return d * normed, d
+
+    norm_sums(back_second, "ln2_gain", "ln2_bias")
     ready("mix")
     column_sums("proj_bias", g, D)
     for span in pieces("w_proj", mix, lambda: g[...], 256):
@@ -1111,17 +1119,14 @@
 
     loop(D // 256, to_attn)
     ready("x")
-    clear("ln1_gain")
-    clear("ln1_bias")
 
     def back_first(i):
         normed, inv = normalize(x[tile(i), :].astype(jnp.float32))
         d = temp[tile(i), :]
-        column_add("ln1_gain", d * normed, False)
-        column_add("ln1_bias", d, False)
         mid[tile(i), :] = mid[tile(i), :] + norm_back(d, normed, inv, vector(table, "ln1_gain"))
-
-    loop(count // 16, back_first)
+        return d * normed, d
+
+    norm_sums(back_first, "ln1_gain", "ln1_bias")
     outs = []
     for b in range(sz.buffers):
         outs.append(
@@ -1213,6 +1218,7 @@
             pltpu.VMEM((sz.total, D), bf),
             pltpu.VMEM((sz.total, D), f32),
             pltpu.VMEM((max(8, sz.full - sz.rows), D), f32),
+            pltpu.VMEM((2, 8, D), f32),
             pltpu.SemaphoreType.DMA((24 + 2 * sz.buffers,)),
             pltpu.SemaphoreType.DMA((2 * sz.buffers,)),
         ],

time: 262 us -> 253 us (0.966)
  Pallas kernels: 254 us -> 245 us
    pallas_call x1, Pallas kernels: 145 us -> 136 us  [backward(): pl.pallas_call(functools.partial(backward_kernel, place, entries, sz), ou...]
where the time goes in v1:
time: 253 us
  Pallas kernels  245 us (97%)
  local copies, waits for them, and re-layouts  7.28 us (3%)
    pallas_call x1, Pallas kernels, backward(): pl.pallas_call(functools.partial(backward_kernel, place, entries, sz), ou...  136 us
    pallas_call x1, Pallas kernels, forward(): pl.pallas_call(functools.partial(forward_kernel, place, entries, sz), out...  109 us

profile of v1, /device:TPU:0, one launch (start us, length us, event | category | flops | bytes accessed | tf_op | source)
XLA Modules:
  0.0 252.7 jit_solution(13546106617071150950)
XLA Ops:
  0.6 1.8 pad_bitcast_fusion.raw
  2.4 109.0 %forward.1 = (bf16[768,2304]{1,0:T(8,128)(2,1)}, bf16[768,768]{1,0:T(8,128)(2,1)}, bf16[768,3072]{1,0:T(8,128)(2,1)}, bf16[3072,768]{1,0:T(8,128)(2,1)}, bf16[41...) custom-call(bf16[1744,128]{1,0:T(8,128)(2,1)} %pad_bitcast_fusion.ra, ...), custom_call_target="tpu_custom_call" | custom-call | tf_op jit(solution)/shard_map/forward/pallas_call | solution.py:890
  111.5 135.8 %backward.1 = (f32[1744,128]{1,0:T(8,128)}, f32[512,768]{1,0:T(8,128)}) custom-call(bf16[512,768]{1,0:T(8,128)(2,1)} %tokens.3, bf16[512,768]{1,0:T(8,128)(2,1)} %cotangent.1, s32[2,2]{1,0:T(2,128)} %lengths.3, f32[16,3072]{1,0:T(8,128)} %get-tuple-element.20.table, bf16[768,2304]{1,0:T(8,128)(2,1)} %get-tuple-element.21.refs_0_, ...), custom_call_target="tpu_custom_call" | custom-call | tf_op jit(solution)/shard_map/backward/pallas_call | solution.py:1191
  247.2 0.0 copy-start
  247.2 2.3 slice.4
  249.5 2.1 copy.9
  251.6 0.0 copy-done
  251.6 1.1 copy.10
Async XLA Ops:
  247.2 4.3 %copy-start = (f32[512,768]{1,0:T(8,128)S(1)}, f32[512,768]{1,0:T(8,128)}, u32[]{:S(2)}) copy-start(f32[512,768]{1,0:T(8,128)} %get-tuple-element.39) | copy-start | bytes 4718596

commit v2 on v0

--- a/solution.py
+++ b/solution.py
@@ -8,9 +8,50 @@
 from jax.experimental.pallas import tpu as pltpu
 from jax.sharding import PartitionSpec as P
 
+ATTN_IN_NAME = "attn_in"
+QKV_NAME = "qkv"
+PROBS_NAME = "probs"
+MIX_NAME = "mix"
+MID_NAME = "mid"
+MLP_IN_NAME = "mlp_in"
+ACT_NAME = "act"
+SLOPE_NAME = "slope"
+LN1_GAIN_NAME = "ln1_gain"
+LN1_BIAS_NAME = "ln1_bias"
+W_QKV_NAME = "w_qkv"
+Q_BIAS_NAME = "q_bias"
+V_BIAS_NAME = "v_bias"
+W_PROJ_NAME = "w_proj"
+PROJ_BIAS_NAME = "proj_bias"
+LN2_GAIN_NAME = "ln2_gain"
+LN2_BIAS_NAME = "ln2_bias"
+W_FC1_NAME = "w_fc1"
+FC1_BIAS_NAME = "fc1_bias"
+W_FC2_NAME = "w_fc2"
+FC2_BIAS_NAME = "fc2_bias"
+G_NAME = "g"
+X_NAME = "x"
+BACKWARD_NAME = "backward"
 AXES = ("dp", "fsdp")
 LANES = 128
 CORE = 3
+MESH = pl.DeviceIdType.MESH
+
+
+def quot(a, b):
+    if isinstance(a, int) and isinstance(b, int):
+        return a // b
+    return a if isinstance(b, int) and b == 1 else lax.div(a, jnp.int32(b))
+
+
+def rest(a, b):
+    if isinstance(a, int) and isinstance(b, int):
+        return a % b
+    return lax.rem(a, jnp.int32(b))
+
+
+def pick(cond, a, b):
+    return lax.select(cond, lax.add(jnp.int32(0), a), lax.add(jnp.int32(0), b))
 
 
 class Place:
@@ -55,7 +96,7 @@
         out = [0, 0, 0, 0]
         for axis in range(2):
             for phys, step, size, stride in self.digits[axis]:
-                out[phys] = out[phys] + ((index[axis] // stride) % size) * step
+                out[phys] = out[phys] + rest(quot(index[axis], stride), size) * step
         return out
 
     def device(self, coords):
@@ -63,7 +104,7 @@
         for axis in range(2):
             total = 0
             for phys, step, size, stride in self.digits[axis]:
-                total = total + ((coords[phys] // step) % size) * stride
+                total = total + rest(quot(coords[phys], step), size) * stride
             out.append(total)
         return tuple(out)
 
@@ -88,7 +129,7 @@
 def flipped(mine, rel, size):
     total, bit = 0, 1
     while bit < size:
-        total = total + bit * (((mine // bit) % 2 + (rel // bit) % 2) % 2)
+        total = total + bit * rest(rest(quot(mine, bit), 2) + rest(quot(rel, bit), 2), 2)
         bit *= 2
     return total
 
@@ -292,7 +333,7 @@
     if size > 2:
         spot = dest[dim]
         if way == 1:
-            spot = spot + jnp.where(at[dim] == dest[dim], size - dest[dim], 0)
+            spot = spot + pick(at[dim] == dest[dim], size - dest[dim], 0)
         index = index * (size + 1) + spot
     return plan[k][0][pos] + index
 
@@ -441,19 +482,19 @@
 INV_ROOT_TWO_PI = 0.3989422804014327
 
 PIECES = (
-    ("ln1_gain", (D,)),
-    ("ln1_bias", (D,)),
-    ("w_qkv", (D, 3 * D)),
-    ("q_bias", (D,)),
-    ("v_bias", (D,)),
-    ("w_proj", (D, D)),
-    ("proj_bias", (D,)),
-    ("ln2_gain", (D,)),
-    ("ln2_bias", (D,)),
-    ("w_fc1", (D, FF)),
-    ("fc1_bias", (FF,)),
-    ("w_fc2", (FF, D)),
-    ("fc2_bias", (D,)),
+    (LN1_GAIN_NAME, (D,)),
+    (LN1_BIAS_NAME, (D,)),
+    (W_QKV_NAME, (D, 3 * D)),
+    (Q_BIAS_NAME, (D,)),
+    (V_BIAS_NAME, (D,)),
+    (W_PROJ_NAME, (D, D)),
+    (PROJ_BIAS_NAME, (D,)),
+    (LN2_GAIN_NAME, (D,)),
+    (LN2_BIAS_NAME, (D,)),
+    (W_FC1_NAME, (D, FF)),
+    (FC1_BIAS_NAME, (FF,)),
+    (W_FC2_NAME, (FF, D)),
+    (FC2_BIAS_NAME, (D,)),
 )
 MATRICES = tuple(name for name, shape in PIECES if len(shape) == 2)
 VECTORS = tuple(name for name, shape in PIECES if len(shape) == 1)
@@ -551,7 +592,7 @@
 
 
 GATHER_SPANS = spans({name: 1 for name in MATRICES})
-SCATTER_SPANS = spans({"w_qkv": 2, "w_proj": 1, "w_fc1": 2, "w_fc2": 2})
+SCATTER_SPANS = spans({W_QKV_NAME: 2, W_PROJ_NAME: 1, W_FC1_NAME: 2, W_FC2_NAME: 2})
 
 
 def stage_rows(spans_, rows):
@@ -721,21 +762,21 @@
 
 
 SCALE = 1.0 / math.sqrt(HEAD_DIM)
-SAVED = ("attn_in", "qkv", "probs", "mix", "mid", "mlp_in", "act", "slope")
+SAVED = (ATTN_IN_NAME, QKV_NAME, PROBS_NAME, MIX_NAME, MID_NAME, MLP_IN_NAME, ACT_NAME, SLOPE_NAME)
 
 
 def saved_shapes(sz):
     t = sz.total
     bf = jnp.bfloat16
     return {
-        "attn_in": ((t, D), bf),
-        "qkv": ((t, 3 * D), bf),
-        "probs": ((sz.buffers * sz.pairs * 2, sz.rows, sz.rows), bf),
-        "mix": ((t, D), bf),
-        "mid": ((t, D), jnp.float32),
-        "mlp_in": ((t, D), bf),
-        "act": ((t, FF), bf),
-        "slope": ((t, FF), bf),
+        ATTN_IN_NAME: ((t, D), bf),
+        QKV_NAME: ((t, 3 * D), bf),
+        PROBS_NAME: ((sz.buffers * sz.pairs * 2, sz.rows, sz.rows), bf),
+        MIX_NAME: ((t, D), bf),
+        MID_NAME: ((t, D), jnp.float32),
+        MLP_IN_NAME: ((t, D), bf),
+        ACT_NAME: ((t, FF), bf),
+        SLOPE_NAME: ((t, FF), bf),
     }
 
 
@@ -775,27 +816,27 @@
         vector_rows(stage, span, margin, table)
         m = MATRICES.index(name)
         pltpu.make_async_copy(w[name], mats[name], done_w.at[m]).start()
-    table[QKV_BIAS : QKV_BIAS + 1, 0:D] = vector(table, "q_bias")
+    table[QKV_BIAS : QKV_BIAS + 1, 0:D] = vector(table, Q_BIAS_NAME)
     table[QKV_BIAS : QKV_BIAS + 1, D : 2 * D] = jnp.zeros((1, D), jnp.float32)
-    table[QKV_BIAS : QKV_BIAS + 1, 2 * D : 3 * D] = vector(table, "v_bias")
+    table[QKV_BIAS : QKV_BIAS + 1, 2 * D : 3 * D] = vector(table, V_BIAS_NAME)
 
     def scale_first(i):
-        a["attn_in"][tile(i), :] = low(
-            normed[tile(i), :] * vector(table, "ln1_gain") + vector(table, "ln1_bias")
+        a[ATTN_IN_NAME][tile(i), :] = low(
+            normed[tile(i), :] * vector(table, LN1_GAIN_NAME) + vector(table, LN1_BIAS_NAME)
         )
 
     loop(sz.total // 16, scale_first)
-    keep("attn_in")
+    keep(ATTN_IN_NAME)
 
     def to_qkv(c):
-        a["qkv"][:, c] = low(
-            dot(a["attn_in"][...], w["w_qkv"][:, c]) + table[QKV_BIAS : QKV_BIAS + 1, c]
+        a[QKV_NAME][:, c] = low(
+            dot(a[ATTN_IN_NAME][...], w[W_QKV_NAME][:, c]) + table[QKV_BIAS : QKV_BIAS + 1, c]
         )
 
     columns(3 * D, 256, to_qkv)
-    keep("qkv")
-
-    qkv, probs, mix = a["qkv"], a["probs"], a["mix"]
+    keep(QKV_NAME)
+
+    qkv, probs, mix = a[QKV_NAME], a[PROBS_NAME], a[MIX_NAME]
     for b in range(sz.buffers):
         rows = sz.at(b)
         seg_r = segments(lengths, b, sz.images, (sz.rows, 1), 0)
@@ -817,47 +858,47 @@
             mix[rows, at(0)] = low(mixed)
 
         loop(sz.pairs, attend)
-    keep("probs")
-    keep("mix")
+    keep(PROBS_NAME)
+    keep(MIX_NAME)
 
     def to_mid(c):
-        made = dot(mix[...], w["w_proj"][:, c]) + table[
-            VECTORS.index("proj_bias") : VECTORS.index("proj_bias") + 1, c
+        made = dot(mix[...], w[W_PROJ_NAME][:, c]) + table[
+            VECTORS.index(PROJ_BIAS_NAME) : VECTORS.index(PROJ_BIAS_NAME) + 1, c
         ]
         for b in range(sz.buffers):
-            a["mid"][sz.at(b), c] = (
+            a[MID_NAME][sz.at(b), c] = (
                 tokens[sz.given(b), c].astype(jnp.float32) + made[sz.at(b), :]
             )
 
     columns(D, 256, to_mid)
-    keep("mid")
+    keep(MID_NAME)
 
     def norm_second(i):
-        a["mlp_in"][tile(i), :] = low(
-            normalize(a["mid"][tile(i), :])[0] * vector(table, "ln2_gain")
-            + vector(table, "ln2_bias")
+        a[MLP_IN_NAME][tile(i), :] = low(
+            normalize(a[MID_NAME][tile(i), :])[0] * vector(table, LN2_GAIN_NAME)
+            + vector(table, LN2_BIAS_NAME)
         )
 
     loop(sz.total // 16, norm_second)
-    keep("mlp_in")
+    keep(MLP_IN_NAME)
 
     def to_act(c):
-        at = VECTORS.index("fc1_bias")
-        pre = dot(a["mlp_in"][...], w["w_fc1"][:, c]) + table[at : at + 1, c]
+        at = VECTORS.index(FC1_BIAS_NAME)
+        pre = dot(a[MLP_IN_NAME][...], w[W_FC1_NAME][:, c]) + table[at : at + 1, c]
         phi = 0.5 * (1.0 + lax.erf(pre * ROOT_HALF))
-        a["act"][:, c] = low(pre * phi)
-        a["slope"][:, c] = low(phi + pre * jnp.exp(-0.5 * pre * pre) * INV_ROOT_TWO_PI)
+        a[ACT_NAME][:, c] = low(pre * phi)
+        a[SLOPE_NAME][:, c] = low(phi + pre * jnp.exp(-0.5 * pre * pre) * INV_ROOT_TWO_PI)
 
     columns(FF, 256, to_act)
-    keep("act")
-    keep("slope")
+    keep(ACT_NAME)
+    keep(SLOPE_NAME)
 
     def to_out(c):
-        at = VECTORS.index("fc2_bias")
-        made = dot(a["act"][...], w["w_fc2"][:, c]) + table[at : at + 1, c]
+        at = VECTORS.index(FC2_BIAS_NAME)
+        made = dot(a[ACT_NAME][...], w[W_FC2_NAME][:, c]) + table[at : at + 1, c]
         for b in range(sz.buffers):
             valid = valid_rows(lengths, b, sz.images, sz.rows)
-            block_out[sz.given(b), c] = low(valid * (a["mid"][sz.at(b), c] + made[sz.at(b), :]))
+            block_out[sz.given(b), c] = low(valid * (a[MID_NAME][sz.at(b), c] + made[sz.at(b), :]))
             if sz.full > sz.rows:
                 block_out[b * sz.full + sz.rows : (b + 1) * sz.full, c] = jnp.zeros(
                     (sz.full - sz.rows, made.shape[1]), jnp.bfloat16
@@ -922,32 +963,32 @@
     me = place.coords()
     margin = own.shape[1]
     count = sz.total
-    order = ("g", "act", "w_fc2", "slope", "mlp_in", "w_fc1", "mid", "mix", "x", "qkv", "probs")
+    order = (G_NAME, ACT_NAME, W_FC2_NAME, SLOPE_NAME, MLP_IN_NAME, W_FC1_NAME, MID_NAME, MIX_NAME, X_NAME, QKV_NAME, PROBS_NAME)
 
     def fetches(name):
         sem = load.at[order.index(name)]
-        if name in ("g", "x"):
-            src, dst = (cotangent, g) if name == "g" else (tokens, x)
+        if name in (G_NAME, X_NAME):
+            src, dst = (cotangent, g) if name == G_NAME else (tokens, x)
             return [
                 pltpu.make_async_copy(
                     src.at[sz.given(b)],
                     dst.at[sz.at(b)],
-                    load.at[order.index(name) if b == 0 else len(order) + 10 + 2 * b + (name == "g")],
+                    load.at[order.index(name) if b == 0 else len(order) + 10 + 2 * b + (name == G_NAME)],
                 )
                 for b in range(sz.buffers)
             ]
         return [pltpu.make_async_copy(*places[name], sem)]
 
     places = {
-        "act": (given["act"], wide),
-        "slope": (given["slope"], slope),
-        "mlp_in": (given["mlp_in"], narrow),
-        "mid": (given["mid"], mid),
-        "mix": (given["mix"], mix),
-        "qkv": (given["qkv"], qkv),
-        "probs": (given["probs"], probs),
-        "w_fc2": (mats["w_fc2"], big_a),
-        "w_fc1": (mats["w_fc1"], big_b),
+        ACT_NAME: (given[ACT_NAME], wide),
+        SLOPE_NAME: (given[SLOPE_NAME], slope),
+        MLP_IN_NAME: (given[MLP_IN_NAME], narrow),
+        MID_NAME: (given[MID_NAME], mid),
+        MIX_NAME: (given[MIX_NAME], mix),
+        QKV_NAME: (given[QKV_NAME], qkv),
+        PROBS_NAME: (given[PROBS_NAME], probs),
+        W_FC2_NAME: (mats[W_FC2_NAME], big_a),
+        W_FC1_NAME: (mats[W_FC1_NAME], big_b),
     }
 
     def begin(name):
@@ -989,18 +1030,18 @@
         lay_vectors(stage, span, margin, sums)
         cut(stage, span, own, entries)
 
-    ready("g")
+    ready(G_NAME)
     for b in range(sz.buffers):
         rows = sz.at(b)
         valid = valid_rows(lengths, b, sz.images, sz.rows)
         g[rows, :] = low(g[rows, :].astype(jnp.float32) * valid)
-    ready("act")
-    column_sums("fc2_bias", g, D)
-    for span in pieces("w_fc2", wide, lambda: g[...], 256):
+    ready(ACT_NAME)
+    column_sums(FC2_BIAS_NAME, g, D)
+    for span in pieces(W_FC2_NAME, wide, lambda: g[...], 256):
         finish(span)
 
-    ready("w_fc2")
-    ready("slope")
+    ready(W_FC2_NAME)
+    ready(SLOPE_NAME)
 
     def to_pre(i):
         c = pl.ds(pl.multiple_of(i * 256, 256), 256)
@@ -1010,32 +1051,32 @@
     loop(FF // 256, to_pre)
     late = [
         pltpu.make_async_copy(
-            mats["w_qkv"].at[:, i * D : (i + 1) * D],
+            mats[W_QKV_NAME].at[:, i * D : (i + 1) * D],
             big_a.at[i * D : (i + 1) * D],
             load.at[len(order) + 8 + i],
         )
         for i in range(3)
     ]
     late.append(
-        pltpu.make_async_copy(mats["w_proj"], big_a.at[3 * D : 4 * D], load.at[len(order) + 11])
+        pltpu.make_async_copy(mats[W_PROJ_NAME], big_a.at[3 * D : 4 * D], load.at[len(order) + 11])
     )
     for c in reversed(late):
         c.start()
-    ready("mlp_in")
-    column_sums("fc1_bias", wide, FF)
-    for span in pieces("w_fc1", narrow, lambda: wide[...], 128):
+    ready(MLP_IN_NAME)
+    column_sums(FC1_BIAS_NAME, wide, FF)
+    for span in pieces(W_FC1_NAME, narrow, lambda: wide[...], 128):
         finish(span)
 
-    attn_load = pltpu.make_async_copy(given["attn_in"], narrow, load.at[len(order) + 7])
+    attn_load = pltpu.make_async_copy(given[ATTN_IN_NAME], narrow, load.at[len(order) + 7])
     attn_load.start()
-    ready("w_fc1")
+    ready(W_FC1_NAME)
 
     def to_mlp(i):
         c = pl.ds(pl.multiple_of(i * 256, 256), 256)
         temp[:, c] = dot(wide[...], big_b[c, :], 1, 1)
 
     loop(D // 256, to_mlp)
-    ready("mid")
+    ready(MID_NAME)
 
     def column_add(name, value, first):
         at = SUMS.index(name)
@@ -1047,22 +1088,22 @@
         at = SUMS.index(name)
         sums[at : at + 1, 0:D] = jnp.zeros((1, D), jnp.float32)
 
-    clear("ln2_gain")
-    clear("ln2_bias")
+    clear(LN2_GAIN_NAME)
+    clear(LN2_BIAS_NAME)
 
     def back_second(i):
         normed, inv = normalize(mid[tile(i), :])
         d = temp[tile(i), :]
-        column_add("ln2_gain", d * normed, False)
-        column_add("ln2_bias", d, False)
-        v = g[tile(i), :].astype(jnp.float32) + norm_back(d, normed, inv, vector(table, "ln2_gain"))
+        column_add(LN2_GAIN_NAME, d * normed, False)
+        column_add(LN2_BIAS_NAME, d, False)
+        v = g[tile(i), :].astype(jnp.float32) + norm_back(d, normed, inv, vector(table, LN2_GAIN_NAME))
         mid[tile(i), :] = v
         g[tile(i), :] = low(v)
 
     loop(count // 16, back_second)
-    ready("mix")
-    column_sums("proj_bias", g, D)
-    for span in pieces("w_proj", mix, lambda: g[...], 256):
+    ready(MIX_NAME)
+    column_sums(PROJ_BIAS_NAME, g, D)
+    for span in pieces(W_PROJ_NAME, mix, lambda: g[...], 256):
         finish(span)
     late[3].wait()
 
@@ -1072,8 +1113,8 @@
         slope[:, c] = low(dot(g[...], big_a[rows, :], 1, 1))
 
     loop(D // 256, to_mix)
-    ready("qkv")
-    ready("probs")
+    ready(QKV_NAME)
+    ready(PROBS_NAME)
     for b in range(sz.buffers):
         rows = sz.at(b)
 
@@ -1110,16 +1151,16 @@
         temp[:, c] = made
 
     loop(D // 256, to_attn)
-    ready("x")
-    clear("ln1_gain")
-    clear("ln1_bias")
+    ready(X_NAME)
+    clear(LN1_GAIN_NAME)
+    clear(LN1_BIAS_NAME)
 
     def back_first(i):
         normed, inv = normalize(x[tile(i), :].astype(jnp.float32))
         d = temp[tile(i), :]
-        column_add("ln1_gain", d * normed, False)
-        column_add("ln1_bias", d, False)
-        mid[tile(i), :] = mid[tile(i), :] + norm_back(d, normed, inv, vector(table, "ln1_gain"))
+        column_add(LN1_GAIN_NAME, d * normed, False)
+        column_add(LN1_BIAS_NAME, d, False)
+        mid[tile(i), :] = mid[tile(i), :] + norm_back(d, normed, inv, vector(table, LN1_GAIN_NAME))
 
     loop(count // 16, back_first)
     outs = []
@@ -1146,10 +1187,10 @@
         sums[len(SUMS) : len(SUMS) + 1, c] = wide_sum
 
     columns(3 * D, 256, qv_sums)
-    for name, part in (("q_bias", 0), ("v_bias", 2)):
+    for name, part in ((Q_BIAS_NAME, 0), (V_BIAS_NAME, 2)):
         at = SUMS.index(name)
         sums[at : at + 1, 0:D] = sums[len(SUMS) : len(SUMS) + 1, part * D : (part + 1) * D]
-    for span in pieces("w_qkv", narrow, lambda: wide[:, 0 : 3 * D], 128):
+    for span in pieces(W_QKV_NAME, narrow, lambda: wide[:, 0 : 3 * D], 128):
         finish(span)
 
     scatter_all(place, me, own, cross, slots, total, (cross_send, cross_recv, send, recv))
@@ -1202,13 +1243,13 @@
             pltpu.VMEM(TABLE, f32),
             pltpu.VMEM((FF, D), bf),
             pltpu.VMEM((D, FF), bf),
-            scratch("act"),
-            scratch("slope"),
-            scratch("qkv"),
-            scratch("probs"),
-            scratch("mix"),
-            scratch("mid"),
-            scratch("mlp_in"),
+            scratch(ACT_NAME),
+            scratch(SLOPE_NAME),
+            scratch(QKV_NAME),
+            scratch(PROBS_NAME),
+            scratch(MIX_NAME),
+            scratch(MID_NAME),
+            scratch(MLP_IN_NAME),
             pltpu.VMEM((sz.total, D), bf),
             pltpu.VMEM((sz.total, D), bf),
             pltpu.VMEM((sz.total, D), f32),
@@ -1219,17 +1260,808 @@
         compiler_params=pltpu.CompilerParams(
             collective_id=1, has_side_effects=True, vmem_limit_bytes=67 * 10**6
         ),
-        name="backward",
+        name=BACKWARD_NAME,
     )(tokens, cotangent, lengths, table, *[mats[m] for m in MATRICES], *[saved[s] for s in SAVED])
     return input_grad, out.reshape(-1)[:entries]
 
 
+class Share:
+    def __init__(self, place, name, depth, width, low):
+        self.name, self.depth, self.half = name, depth, width // 2
+        self.high = depth // place.chips
+        self.low = low
+        self.rows = self.high * (width // LANES)
+        third = self.high // 3
+        if name is None:
+            self.parts = {2: (0, self.high, 0, self.half)}
+        elif third % 32:
+            first = -(-self.half // LANES // 2) * LANES
+            self.parts = {
+                2: (0, third, 0, self.half),
+                3: (third, third, 0, self.half),
+                0: (2 * third, third, 0, first),
+                1: (2 * third, third, first, self.half - first),
+            }
+        else:
+            self.parts = {
+                2: (0, third, 0, self.half),
+                3: (third, third, 0, self.half),
+                0: (2 * third, third // 2, 0, self.half),
+                1: (2 * third + third // 2, third // 2, 0, self.half),
+            }
+
+
+def shares(place):
+    out = [Share(place, n, *SHAPES[n], BASES[n]) for n in MATRICES]
+    return out + [Share(place, None, 16 * place.chips, 2 * LANES, None)]
+
+
+VECTOR_LIST = [(n, j) for n in VECTORS for j in range(SHAPES[n][0] // LANES)]
+
+
+def fits(place):
+    return place.size == [2, 2, 4, 2]
+
+
+def block_of(place, coords):
+    return (coords[1] * 2 + coords[0]) * 4 + coords[2]
+
+
+def chip_of(block):
+    return [rest(quot(block, 4), 2), quot(block, 8), rest(block, 4)]
+
+
+class Summing:
+    def __init__(self, place, me, parts, own, cross, slots, send, recv, cross_send, cross_recv):
+        self.place, self.me, self.parts = place, me, parts
+        self.own, self.cross, self.slots = own, cross, slots
+        self.send, self.recv = send, recv
+        self.cross_send, self.cross_recv = cross_send, cross_recv
+        self.plan = slot_plan(place, 16 * sum(place.shares))
+        self.slot, self.sent = 0, []
+        self.waits, self.then, self.left = {}, {}, {}
+
+    def rect(self, p, k, dest):
+        top, high, left, wide = self.parts[p].parts[k]
+        row = block_of(self.place, dest) * self.parts[p].high + top
+        return pl.multiple_of(row, 16), high, left, wide
+
+    def swap(self, p, first, count, chunk):
+        rows = pl.ds(pl.multiple_of(first, 16), count)
+        return pltpu.make_async_remote_copy(
+            src_ref=self.own[p].at[1 - self.me[CORE], rows, :],
+            dst_ref=self.cross[p].at[rows, :],
+            send_sem=self.cross_send.at[p, chunk],
+            recv_sem=self.cross_recv.at[p, chunk],
+            device_id=self.place.device(partner(self.me)),
+            device_id_type=MESH,
+        )
+
+    def hand(self, p, k, pos, way, dest, to):
+        row, high, left, wide = self.rect(p, k, dest)
+        slot = slot_of(self.place, self.plan, k, pos, way, to, dest)
+        return pltpu.make_async_remote_copy(
+            src_ref=self.own[p].at[self.me[CORE], pl.ds(row, high), pl.ds(left, wide)],
+            dst_ref=self.slots[p][k].at[slot],
+            send_sem=self.send.at[p, k, self.place.chip(dest)],
+            recv_sem=self.recv[p][k].at[slot],
+            device_id=self.place.device(to),
+            device_id_type=MESH,
+        )
+
+    def parents(self, k, rel, dest):
+        order = self.place.orders[k]
+        for pos in range(2, -1, -1):
+            dim = order[pos]
+            if rel[dim] == 0:
+                continue
+            if self.place.size[dim] == 2:
+                other = list(self.me)
+                other[dim] = 1 - other[dim]
+                return [(True, pos, 0, other)]
+            here, there = self.me[dim], dest[dim]
+            return [
+                (here > there, pos, 0, moved(self.me, dim, -1)),
+                (here < there, pos, 1, moved(self.me, dim, 1)),
+            ]
+        return []
+
+    def aim(self, x, y, turn):
+        z = self.me[2]
+        inner = pick(z >= 2, 3 - z, z)
+        end, middle = TURNS[0][turn], TURNS[1][turn]
+        at = pick(inner == 0, end, middle)
+        dest = [
+            1 - self.me[0] if x else self.me[0],
+            1 - self.me[1] if y else self.me[1],
+            pick(z >= 2, 3 - at, at),
+        ]
+        cond = inner == 0 if turn == 0 else inner == 1 if turn == 3 else True
+        if turn == 4:
+            dest[2] = z
+        return cond, dest + [self.me[CORE]]
+
+    def task(self, p, k, rel, dest):
+        row, high, left, wide = self.rect(p, k, dest)
+        core = self.me[CORE]
+        cols = slice(left, left + wide)
+
+        def add(terms):
+            for i in range(high // 16):
+                rows = pl.ds(pl.multiple_of(row + i * 16, 16), 16)
+                value = self.own[p][core, rows, cols].astype(jnp.float32)
+                for term in terms:
+                    value = value + term(i, rows).astype(jnp.float32)
+                self.own[p][core, rows, cols] = low(value)
+
+        def kid(pos, way):
+            slot = slot_of(self.place, self.plan, k, pos, way, self.me, dest)
+            return lambda i, rows: self.slots[p][k][slot, i * 16 : (i + 1) * 16, :]
+
+        kids = onward(self.place, self.place.orders[k], self.me, rel, dest)
+        sure = [(pos, way) for cond, pos, way, _ in kids if cond is True]
+        for pos, way in sure:
+            self.hand(p, k, pos, way, dest, self.me).wait_recv()
+        add([lambda i, rows: self.cross[p][rows, cols]] + [kid(*s) for s in sure])
+        for cond, pos, way, _ in kids:
+            if cond is True or cond is False:
+                continue
+
+            def take(pos=pos, way=way):
+                self.hand(p, k, pos, way, dest, self.me).wait_recv()
+                add([kid(pos, way)])
+
+            pl.when(cond)(take)
+        for cond, pos, way, to in self.parents(k, rel, dest):
+            when(cond, lambda: self.hand(p, k, pos, way, dest, to).start())
+
+    def offer(self, p, waits, then):
+        self.waits[p], self.then[p] = waits, then
+        self.left[p] = len(self.parts[p].parts)
+
+    def step(self, p, k, x, y, turn):
+        if p in self.waits:
+            self.waits.pop(p)()
+        cond, dest = self.aim(x, y, turn)
+        rel = (x, y, 0 if turn == 4 else 1)
+        when(cond, lambda: self.task(p, k, rel, dest))
+        self.sent.append((p, k, x, y, turn))
+        if x == y == 0 and turn == 4:
+            self.left[p] -= 1
+            if not self.left[p]:
+                self.then[p]()
+
+    def pump(self):
+        self.slot += 1
+        last = self.slot == len(SCHEDULE) - 1
+        early, self.sent = (self.sent, []) if last else ([], self.sent)
+        for code in SCHEDULE[self.slot]:
+            p, k = len(MATRICES) - 1 - code // 80, (code // 20) % 4
+            x, y, turn = (code // 10) % 2, (code // 5) % 2, code % 5
+            self.step(p, k, x, y, turn)
+            if p == 0 and k == 2:
+                self.step(len(MATRICES), k, x, y, turn)
+            for one in early[:4]:
+                self.ended(*one)
+            early = early[4:]
+        self.sent = early + self.sent
+
+    def ended(self, p, k, x, y, turn):
+        known, dest = self.aim(x, y, turn)
+
+        def wait():
+            rel = (x, y, 0 if turn == 4 else 1)
+            for cond, pos, way, to in self.parents(k, rel, dest):
+                when(cond, lambda: self.hand(p, k, pos, way, dest, to).wait_send())
+
+        if (x, y, turn) != (0, 0, 4):
+            when(known, wait)
+
+    def drain(self):
+        for one in self.sent:
+            self.ended(*one)
+
+
+def most_blocks(part, entries):
+    return ((entries + 2 * LANES) // LANES - 1) // part.rows + 2
+
+
+def meeting(part, entries, block):
+    start = (part.low + block * part.rows) * LANES
+    return quot(start, entries), quot(start + part.rows * LANES - 1, entries)
+
+
+def first_block(part, entries, flat):
+    ahead = entries * flat - part.low * LANES
+    return quot(pick(ahead > 0, ahead, 0), part.rows * LANES)
+
+
+def deliver(place, me, parts, own, land, land_send, land_recv, vec_land, vec_send, vec_recv, local, entries):
+    flat, core = place.flat(me), me[CORE]
+    mine = block_of(place, me)
+    devices = place.devices
+
+    def device(d):
+        return (quot(d, place.shape[1]), rest(d, place.shape[1]))
+
+    def block_copy(p, block, to, which):
+        part = parts[p]
+        slot = block - first_block(part, entries, to)
+        return pltpu.make_async_remote_copy(
+            src_ref=own[p].at[core, pl.ds(pl.multiple_of(block * part.high, 16), part.high), :],
+            dst_ref=land[p].at[slot, core],
+            send_sem=land_send.at[p, which],
+            recv_sem=land_recv[p].at[slot, core],
+            device_id=device(to),
+            device_id_type=MESH,
+        )
+
+    def block_local(p, block):
+        part = parts[p]
+        slot = block - first_block(part, entries, flat)
+        return pltpu.make_async_copy(
+            own[p].at[core, pl.ds(pl.multiple_of(block * part.high, 16), part.high), :],
+            land[p].at[slot, core],
+            local.at[p],
+        )
+
+    def sends(p):
+        one, two = meeting(parts[p], entries, mine)
+        return [
+            (one != flat, one, 0),
+            (jnp.logical_and(two != one, two != flat), two, 1),
+        ], pick(one == flat, 1, pick(two == flat, 1, 0)) > 0
+
+    def vector_pairs():
+        out = []
+        for v, (name, j) in enumerate(VECTOR_LIST):
+            row = BASES[name] + j
+            for d in range((row * LANES) // entries, ((row + 1) * LANES - 1) // entries + 1):
+                if (v // 16, d) not in out:
+                    out.append((v // 16, d))
+        return out
+
+    def vector_copy(n, block, d):
+        return pltpu.make_async_remote_copy(
+            src_ref=own[4].at[0, block * 16 : (block + 1) * 16, :],
+            dst_ref=vec_land.at[block],
+            send_sem=vec_send.at[n],
+            recv_sem=vec_recv.at[block],
+            device_id=device(d),
+            device_id_type=MESH,
+        )
+
+    def start(p):
+        remote, here = sends(p)
+        for cond, to, which in remote:
+            pl.when(cond)(lambda: block_copy(p, mine, to, which).start())
+        pl.when(here)(lambda: block_local(p, mine).start())
+
+    def start_vectors():
+        for n, (block, d) in enumerate(vector_pairs()):
+            home = place.flat(chip_of(block) + [0])
+            if home == d:
+
+                @pl.when(flat == d)
+                def _():
+                    vec_land[block] = own[4][0, block * 16 : (block + 1) * 16, :]
+
+            else:
+                pl.when(flat == home)(lambda: vector_copy(n, block, d).start())
+
+    def expected(p):
+        part = parts[p]
+        low_block = first_block(part, entries, flat)
+        top = part.low + part.rows * place.chips
+        begins = part.low * LANES < entries * (flat + 1)
+        ends = top * LANES > entries * flat
+        for i in range(min(most_blocks(part, entries), place.chips)):
+            block = low_block + i
+            inside = (part.low + block * part.rows) * LANES < entries * (flat + 1)
+            yield both_all(begins, ends, inside, block < place.chips), block, i
+
+    def both_all(*conds):
+        return functools.reduce(jnp.logical_and, conds)
+
+    def finish(stage, margin, out):
+        base = quot(entries * flat, LANES)
+        for p in (3, 2, 1, 0):
+            part = parts[p]
+            blocks = 2 * part.half // LANES
+            remote, here = sends(p)
+            pl.when(here)(lambda: block_local(p, mine).wait())
+            for cond, block, i in expected(p):
+
+                def take():
+                    for half in range(2):
+                        source = place.flat(chip_of_traced(block) + [half])
+
+                        @pl.when(source != flat)
+                        def _():
+                            pltpu.make_async_remote_copy(
+                                src_ref=land[p].at[i, half],
+                                dst_ref=land[p].at[i, half],
+                                send_sem=land_send.at[p, 0],
+                                recv_sem=land_recv[p].at[i, half],
+                                device_id=device(source),
+                                device_id_type=MESH,
+                            ).wait_recv()
+
+                    at = part.low + block * part.rows - base + margin
+                    for r in range(part.high // 16):
+                        for half in range(2):
+                            for j in range(blocks // 2):
+                                stage[
+                                    pl.ds(
+                                        at + r * 16 * blocks + half * (blocks // 2) + j,
+                                        16,
+                                        stride=blocks,
+                                    ),
+                                    :,
+                                ] = land[p][
+                                    i, half, r * 16 : (r + 1) * 16, j * LANES : (j + 1) * LANES
+                                ].astype(jnp.float32)
+
+                pl.when(cond)(take)
+        for n, (block, d) in enumerate(vector_pairs()):
+            home = place.flat(chip_of(block) + [0])
+
+            @pl.when(flat == d)
+            def _():
+                if home != d:
+                    vector_copy(n, block, d).wait_recv()
+                for v in range(block * 16, min((block + 1) * 16, len(VECTOR_LIST))):
+                    name, j = VECTOR_LIST[v]
+                    row = BASES[name] + j
+                    if (row * LANES) // entries <= d <= ((row + 1) * LANES - 1) // entries:
+                        spot = row - (entries * d) // LANES + margin
+                        stage[spot : spot + 1, :] = vec_land[block][
+                            v % 16 : v % 16 + 1, :
+                        ].astype(jnp.float32)
+
+        shift = rest(entries * flat, LANES)
+        back = rest(LANES - shift, LANES)
+        rows = out.shape[0]
+
+        def turn(i):
+            at = pl.ds(pl.multiple_of(margin + i * 16, 16), 16)
+            stage[at, :] = pltpu.roll(stage[at, :], back, 1)
+
+        loop(rows // 16 + 1, turn, 8)
+
+        def merge(i):
+            lane = lax.broadcasted_iota(jnp.int32, (16, LANES), 1)
+            now = stage[pl.ds(margin + i * 16, 16), :]
+            after = stage[pl.ds(margin + i * 16 + 1, 16), :]
+            out[tile(i), :] = jnp.where(lane < LANES - shift, now, after)
+
+        loop(rows // 16, merge, 8)
+        for p in range(4):
+            for cond, to, which in sends(p)[0]:
+                pl.when(cond)(lambda: block_copy(p, mine, to, which).wait_send())
+        for n, (block, d) in enumerate(vector_pairs()):
+            home = place.flat(chip_of(block) + [0])
+            if home != d:
+                pl.when(flat == home)(lambda: vector_copy(n, block, d).wait_send())
+
+    return start, start_vectors, finish
+
+
+def chip_of_traced(block):
+    return [rest(quot(block, 4), 2), quot(block, 8), rest(block, 4)]
+
+
+SCHEDULE = (
+        (),
+        (),
+        (),
+        (76, 48, 71),
+        (45,),
+        (75, 70),
+        (55,),
+        (56, 65),
+        (115, 87, 136, 85),
+        (46, 95, 135, 150, 126, 125, 33),
+        (60, 72, 155, 86, 151, 116, 50),
+        (5, 127, 40, 35, 78, 130, 97),
+        (154, 51, 61, 99, 120, 128),
+        (145, 32, 105, 158, 215),
+        (159, 90, 49, 98, 15, 66, 112, 88),
+        (210, 114, 110, 140, 59, 58, 217, 77, 156),
+        (138, 195, 25, 235, 17),
+        (111, 16, 73, 131, 121, 62, 96, 19, 230),
+        (137, 47, 119, 216, 178, 6, 146),
+        (57, 41, 7, 238, 157, 207, 237, 68, 206, 152, 205, 79),
+        (141, 219, 233, 118, 122, 218, 139, 193, 225, 67, 37, 236),
+        (133, 39, 30, 220, 10, 209, 9),
+        (132, 147, 113, 91, 8, 231, 52, 74, 42, 80, 36),
+        (53, 200, 117, 199, 92, 134, 69, 221),
+        (106, 142, 173, 0, 232, 38, 108, 100, 153),
+        (208, 109, 129, 12, 20, 226, 175, 93, 201, 185, 63, 211, 18, 190),
+        (11, 222, 107, 223, 176, 81, 196, 26, 31, 43, 179, 168, 101, 197, 278, 191, 28, 166, 227,
+     310, 277, 256, 212, 13, 255, 228, 198, 257, 82, 295, 258, 273, 275, 234, 271, 296, 1, 123, 313,
+     315, 21, 270, 285, 102, 187, 103, 170, 165, 29, 318, 64, 276, 14, 300, 245, 188, 286, 316, 317,
+     203, 239, 2, 169, 250, 311, 298, 252, 279, 23, 290, 192, 305, 3, 180, 83, 265, 186, 177, 202,
+     171, 27, 251, 160, 89, 280, 291, 248, 148, 297, 306, 194, 260, 172, 167, 319, 259, 94, 247,
+     229, 181, 281, 240, 34, 253, 288, 246, 312, 266, 307, 213, 254, 149, 22, 268, 299, 224, 143,
+     274, 161, 272, 182, 301, 241, 124, 214, 292, 293, 287, 174, 261, 308, 54, 162, 267, 183, 289,
+     189, 249, 24, 163, 283, 269, 302, 84, 303, 242, 104, 314, 144, 282, 243, 204, 309, 294, 262,
+     263, 4, 44, 184, 164, 244, 304, 284, 264),
+)
+TURNS = ((3, 2, 1, 3, 0), (3, 3, 2, 0, 1))
+
+
+def stage_margin(parts):
+    return max(part.rows for part in parts[:4]) + 16
+
+
+def even_kernel(place, entries, sz, tokens, cotangent, lengths, table, *refs):
+    mats, refs = dict(zip(MATRICES, refs[:4])), refs[4:]
+    given, refs = dict(zip(SAVED, refs[:8])), refs[8:]
+    out, input_grad, refs = refs[0], refs[1], refs[2:]
+    parts = shares(place)
+    own, cross, land, refs = refs[:5], refs[5:10], refs[10:14], refs[14:]
+    slots, recv = [], []
+    for part in parts:
+        slots.append(dict(zip(part.parts, refs)))
+        refs = refs[len(part.parts) :]
+    for part in parts:
+        recv.append(dict(zip(part.parts, refs)))
+        refs = refs[len(part.parts) :]
+    send, cross_send, cross_recv, land_send, refs = *refs[:4], refs[4:]
+    land_recv, refs = refs[:4], refs[4:]
+    vec_land, vec_send, vec_recv, local, refs = *refs[:4], refs[4:]
+    stage, sums, refs = refs[0], refs[1], refs[2:]
+    big_a, big_b, refs = refs[0], refs[1], refs[2:]
+    wide, slope, qkv, probs, mix, mid, narrow, x, g, temp, blank, partial, load, done = refs
+    me = place.coords()
+    flat = place.flat(me)
+    count = sz.total
+    order = (G_NAME, ACT_NAME, W_FC2_NAME, SLOPE_NAME, MLP_IN_NAME, W_FC1_NAME, MID_NAME, MIX_NAME, X_NAME, QKV_NAME, PROBS_NAME)
+
+    def fetches(name):
+        sem = load.at[order.index(name)]
+        if name in (G_NAME, X_NAME):
+            src, dst = (cotangent, g) if name == G_NAME else (tokens, x)
+            return [
+                pltpu.make_async_copy(
+                    src.at[sz.given(b)],
+                    dst.at[sz.at(b)],
+                    load.at[order.index(name) if b == 0 else len(order) + 10 + 2 * b + (name == G_NAME)],
+                )
+                for b in range(sz.buffers)
+            ]
+        return [pltpu.make_async_copy(*places[name], sem)]
+
+    places = {
+        ACT_NAME: (given[ACT_NAME], wide),
+        SLOPE_NAME: (given[SLOPE_NAME], slope),
+        MLP_IN_NAME: (given[MLP_IN_NAME], narrow),
+        MID_NAME: (given[MID_NAME], mid),
+        MIX_NAME: (given[MIX_NAME], mix),
+        QKV_NAME: (given[QKV_NAME], qkv),
+        PROBS_NAME: (given[PROBS_NAME], probs),
+        W_FC2_NAME: (mats[W_FC2_NAME], big_a),
+        W_FC1_NAME: (mats[W_FC1_NAME], big_b),
+    }
+
+    def begin(name):
+        for c in fetches(name):
+            c.start()
+
+    def ready(name):
+        for c in fetches(name):
+            c.wait()
+
+    for name in order:
+        begin(name)
+    barrier = pltpu.get_barrier_semaphore()
+
+    def hello(d):
+        @pl.when(d != flat)
+        def _():
+            pl.semaphore_signal(
+                barrier,
+                inc=1,
+                device_id=(quot(d, place.shape[1]), rest(d, place.shape[1])),
+                device_id_type=MESH,
+            )
+
+    loop(place.devices, hello)
+    adding = Summing(
+        place, me, parts, own, cross, slots, send, recv, cross_send, cross_recv
+    )
+    start, start_vectors, finish = deliver(
+        place, me, parts, own, land, land_send, land_recv, vec_land, vec_send, vec_recv, local, entries
+    )
+
+    def stepped(steps, body, groups):
+        each = steps // groups
+        for n in range(groups):
+            loop(each, lambda i: body(n * each + i))
+            adding.pump()
+
+    def sum_to(name, c, value):
+        at = SUMS.index(name)
+        sums[at : at + 1, c] = value
+
+    def ones():
+        return jnp.ones((8, count), jnp.bfloat16)
+
+    def column_sums(name, ref, width):
+        def body(c):
+            sum_to(name, c, dot(ones(), ref[:, c])[0:1, :])
+
+        columns(width, 256, body)
+
+    def pieces(name, left, right, block, groups):
+        p = MATRICES.index(name)
+        half = parts[p].half
+        steps = parts[p].depth // block
+
+        def body(i):
+            first = pl.multiple_of(i * block, block)
+            value = low(dot(left[:, pl.ds(first, block)], right(), 0, 0))
+            own[p][0, pl.ds(first, block), :] = value[:, :half]
+            own[p][1, pl.ds(first, block), :] = value[:, half:]
+            adding.swap(p, first, block, i).start()
+
+        waits = lambda: loop(steps, lambda i: adding.swap(p, i * block, block, i).wait_recv())
+        adding.offer(p, waits, lambda: start(p))
+        stepped(steps, body, groups)
+        swaps.append((p, steps, block))
+
+    swaps = []
+
+    ready(G_NAME)
+    for b in range(sz.buffers):
+        rows = sz.at(b)
+        valid = valid_rows(lengths, b, sz.images, sz.rows)
+        g[rows, :] = low(g[rows, :].astype(jnp.float32) * valid)
+    ready(ACT_NAME)
+    column_sums(FC2_BIAS_NAME, g, D)
+    pl.semaphore_wait(barrier, place.devices - 1)
+    pieces(W_FC2_NAME, wide, lambda: g[...], 256, 1)
+
+    ready(W_FC2_NAME)
+    ready(SLOPE_NAME)
+
+    def to_pre(i):
+        c = pl.ds(pl.multiple_of(i * 256, 256), 256)
+        made = dot(g[...], big_a[c, :], 1, 1)
+        wide[:, c] = low(made * slope[:, c].astype(jnp.float32))
+
+    stepped(FF // 256, to_pre, 3)
+    late = [
+        pltpu.make_async_copy(
+            mats[W_QKV_NAME].at[:, i * D : (i + 1) * D],
+            big_a.at[i * D : (i + 1) * D],
+            load.at[len(order) + 8 + i],
+        )
+        for i in range(3)
+    ]
+    late.append(
+        pltpu.make_async_copy(mats[W_PROJ_NAME], big_a.at[3 * D : 4 * D], load.at[len(order) + 11])
+    )
+    for c in reversed(late):
+        c.start()
+    ready(MLP_IN_NAME)
+    column_sums(FC1_BIAS_NAME, wide, FF)
+    pieces(W_FC1_NAME, narrow, lambda: wide[...], 128, 3)
+
+    attn_load = pltpu.make_async_copy(given[ATTN_IN_NAME], narrow, load.at[len(order) + 7])
+    attn_load.start()
+    ready(W_FC1_NAME)
+
+    def to_mlp(i):
+        c = pl.ds(pl.multiple_of(i * 256, 256), 256)
+        temp[:, c] = dot(wide[...], big_b[c, :], 1, 1)
+
+    stepped(D // 256, to_mlp, 3)
+    ready(MID_NAME)
+
+    def folded(v):
+        return v[0:8, :] + v[8:16, :]
+
+    def norm_sums(body, gain, bias):
+        partial[...] = jnp.zeros(partial.shape, jnp.float32)
+
+        def step(i):
+            for which, value in enumerate(body(i)):
+                partial[which] += folded(value)
+
+        loop(count // 16, step, 2)
+        for which, name in enumerate((gain, bias)):
+            at = SUMS.index(name)
+            sums[at : at + 1, 0:D] = jnp.sum(partial[which], axis=0, keepdims=True)
+
+
+    def back_second(i):
+        normed, inv = normalize(mid[tile(i), :])
+        d = temp[tile(i), :]
+        v = g[tile(i), :].astype(jnp.float32) + norm_back(d, normed, inv, vector(table, LN2_GAIN_NAME))
+        mid[tile(i), :] = v
+        g[tile(i), :] = low(v)
+        return d * normed, d
+
+    norm_sums(back_second, LN2_GAIN_NAME, LN2_BIAS_NAME)
+    ready(MIX_NAME)
+    column_sums(PROJ_BIAS_NAME, g, D)
+    adding.pump()
+    pieces(W_PROJ_NAME, mix, lambda: g[...], 256, 1)
+    late[3].wait()
+
+    def to_mix(i):
+        c = pl.ds(pl.multiple_of(i * 256, 256), 256)
+        rows = pl.ds(pl.multiple_of(3 * D + i * 256, 256), 256)
+        slope[:, c] = low(dot(g[...], big_a[rows, :], 1, 1))
+
+    stepped(D // 256, to_mix, 1)
+    ready(QKV_NAME)
+    ready(PROBS_NAME)
+    for b in range(sz.buffers):
+        rows = sz.at(b)
+
+        def attend(p):
+            halves = half_lanes(sz.rows)
+            at = lambda part: pl.ds(pl.multiple_of(part * D + p * LANES, LANES), LANES)
+            q, k, v = (qkv[rows, at(part)] for part in range(3))
+            dm = slope[rows, at(0)]
+            dq = dk = dv = 0.0
+            for h in range(2):
+                pr = probs[(b * sz.pairs + p) * 2 + h]
+                dmh = dm * halves[h]
+                dp = dot(dmh, v, 1, 1)
+                prf = pr.astype(jnp.float32)
+                ds = low(prf * (dp - jnp.sum(prf * dp, axis=-1, keepdims=True)))
+                dv = dv + dot(pr, dmh, 0, 0)
+                dq = dq + dot(ds, k * halves[h])
+                dk = dk + dot(ds, q * halves[h], 0, 0)
+            wide[rows, at(0)] = low(dq * SCALE)
+            wide[rows, at(1)] = low(dk * SCALE)
+            wide[rows, at(2)] = low(dv)
+
+        stepped(sz.pairs, attend, 3)
+    for c in late[:3]:
+        c.wait()
+
+    def to_attn(i):
+        c = pl.ds(pl.multiple_of(i * 256, 256), 256)
+        made = None
+        for part in range(3):
+            rows = pl.ds(pl.multiple_of(part * D + i * 256, 256), 256)
+            term = dot(wide[:, part * D : (part + 1) * D], big_a[rows, :], 1, 1)
+            made = term if made is None else made + term
+        temp[:, c] = made
+
+    stepped(D // 256, to_attn, 3)
+    ready(X_NAME)
+
+    def back_first(i):
+        normed, inv = normalize(x[tile(i), :].astype(jnp.float32))
+        d = temp[tile(i), :]
+        mid[tile(i), :] = mid[tile(i), :] + norm_back(d, normed, inv, vector(table, LN1_GAIN_NAME))
+        return d * normed, d
+
+    norm_sums(back_first, LN1_GAIN_NAME, LN1_BIAS_NAME)
+    outs = []
+    for b in range(sz.buffers):
+        outs.append(
+            pltpu.make_async_copy(mid.at[sz.at(b)], input_grad.at[sz.given(b)], done.at[2 * b])
+        )
+        if sz.full > sz.rows:
+            blank[...] = jnp.zeros(blank.shape, blank.dtype)
+            outs.append(
+                pltpu.make_async_copy(
+                    blank,
+                    input_grad.at[b * sz.full + sz.rows : (b + 1) * sz.full],
+                    done.at[2 * b + 1],
+                )
+            )
+    for c in outs:
+        c.start()
+
+    attn_load.wait()
+
+    def qv_sums(c):
+        wide_sum = dot(ones(), wide[:, c])[0:1, :]
+        sums[len(SUMS) : len(SUMS) + 1, c] = wide_sum
+
+    columns(3 * D, 256, qv_sums)
+    for name, part in ((Q_BIAS_NAME, 0), (V_BIAS_NAME, 2)):
+        at = SUMS.index(name)
+        sums[at : at + 1, 0:D] = sums[len(SUMS) : len(SUMS) + 1, part * D : (part + 1) * D]
+    own[4][...] = jnp.zeros(own[4].shape, own[4].dtype)
+    padded = round_up(len(VECTOR_LIST), 16)
+    for v, (name, j) in enumerate(VECTOR_LIST):
+        at = SUMS.index(name)
+        stage[v : v + 1, :] = sums[at : at + 1, j * LANES : (j + 1) * LANES]
+    stage[len(VECTOR_LIST) : padded, :] = jnp.zeros((padded - len(VECTOR_LIST), LANES), jnp.float32)
+    own[4][0, 0:padded, :] = low(stage[0:padded, :])
+    adding.swap(4, 0, parts[4].depth, 0).start()
+    swaps.append((4, 1, parts[4].depth))
+    adding.offer(4, lambda: adding.swap(4, 0, parts[4].depth, 0).wait_recv(), start_vectors)
+    adding.pump()
+    pieces(W_QKV_NAME, narrow, lambda: wide[:, 0 : 3 * D], 128, 3)
+    finish(stage, stage_margin(parts), out)
+    adding.drain()
+    for p, steps, block in swaps:
+        loop(steps, lambda i: adding.swap(p, i * block, block, i).wait_send())
+    for c in outs:
+        c.wait()
+
+
+def even_backward(place, tokens, cotangent, lengths, mats, saved, table, entries):
+    rows = part_rows(entries)
+    sz = Sizes(tokens, lengths)
+    parts = shares(place)
+    dma = pltpu.SemaphoreType.DMA
+    plan = slot_plan(place, rows)
+    rects = [(part, k) for part in parts for k in part.parts]
+    any_spec = pl.BlockSpec(memory_space=pl.ANY)
+    vmem = pl.BlockSpec(memory_space=pltpu.VMEM)
+    smem = pl.BlockSpec(memory_space=pltpu.SMEM)
+    bf, f32 = jnp.bfloat16, jnp.float32
+    shapes = saved_shapes(sz)
+    scratch = lambda name: pltpu.VMEM(*shapes[name])
+    out, input_grad = pl.pallas_call(
+        functools.partial(even_kernel, place, entries, sz),
+        out_shape=[
+            jax.ShapeDtypeStruct((rows, LANES), f32),
+            jax.ShapeDtypeStruct(tokens.shape, f32),
+        ],
+        in_specs=[any_spec, any_spec, smem, vmem] + [any_spec] * 12,
+        out_specs=[vmem, any_spec],
+        scratch_shapes=[pltpu.VMEM((2, part.depth, part.half), bf) for part in parts]
+        + [pltpu.VMEM((part.depth, part.half), bf) for part in parts]
+        + [
+            pltpu.VMEM((most_blocks(part, entries), 2, part.high, part.half), bf)
+            for part in parts[:4]
+        ]
+        + [
+            pltpu.VMEM((plan[k][1], part.parts[k][1], part.parts[k][3]), bf) for part, k in rects
+        ]
+        + [dma((plan[k][1],)) for _, k in rects]
+        + [dma((5, place.classes, place.chips)), dma((5, 12)), dma((5, 12)), dma((4, 2))]
+        + [dma((most_blocks(part, entries), 2)) for part in parts[:4]]
+        + [
+            pltpu.VMEM((-(-len(VECTOR_LIST) // 16), 16, LANES), bf),
+            dma((32,)),
+            dma((-(-len(VECTOR_LIST) // 16),)),
+            dma((4,)),
+            pltpu.VMEM((2 * stage_margin(parts) + rows + 32, LANES), f32),
+            pltpu.VMEM(TABLE, f32),
+            pltpu.VMEM((FF, D), bf),
+            pltpu.VMEM((D, FF), bf),
+            scratch(ACT_NAME),
+            scratch(SLOPE_NAME),
+            scratch(QKV_NAME),
+            scratch(PROBS_NAME),
+            scratch(MIX_NAME),
+            scratch(MID_NAME),
+            scratch(MLP_IN_NAME),
+            pltpu.VMEM((sz.total, D), bf),
+            pltpu.VMEM((sz.total, D), bf),
+            pltpu.VMEM((sz.total, D), f32),
+            pltpu.VMEM((max(8, sz.full - sz.rows), D), f32),
+            pltpu.VMEM((2, 8, D), f32),
+            pltpu.SemaphoreType.DMA((24 + 2 * sz.buffers,)),
+            pltpu.SemaphoreType.DMA((2 * sz.buffers,)),
+        ],
+        compiler_params=pltpu.CompilerParams(
+            collective_id=1, has_side_effects=True, vmem_limit_bytes=67 * 10**6
+        ),
+        name=BACKWARD_NAME,
+    )(tokens, cotangent, lengths, table, *[mats[m] for m in MATRICES], *[saved[s] for s in SAVED])
+    return input_grad, out.reshape(-1)[:entries]
+
+
 def solution(mesh):
     place = Place(mesh)
 
     def shards(tokens, cotangent, params, lengths):
         mats, saved, table, out = forward(place, tokens, params, lengths)
-        input_grad, grad = backward(
+        input_grad, grad = (even_backward if fits(place) else backward)(
             place, tokens, cotangent, lengths, mats, saved, table, params.shape[0]
         )
         return out, input_grad, grad

time: 262 us -> 230 us (0.88)
  Pallas kernels: 254 us -> 222 us
    pallas_call x1, Pallas kernels: 145 us -> 113 us  [even_backward(): pl.pallas_call(functools.partial(even_kernel, place, entries, sz), out_sh...]
where the time goes in v2:
time: 230 us
  Pallas kernels  222 us (97%)
  local copies, waits for them, and re-layouts  7.28 us (3%)
    pallas_call x1, Pallas kernels, even_backward(): pl.pallas_call(functools.partial(even_kernel, place, entries, sz), out_sh...  113 us
    pallas_call x1, Pallas kernels, forward(): pl.pallas_call(functools.partial(forward_kernel, place, entries, sz), out...  109 us

profile of v2, /device:TPU:0, one launch (start us, length us, event | category | flops | bytes accessed | tf_op | source)
XLA Modules:
  0.0 229.7 jit_solution(5768007090321748189)
XLA Ops:
  0.6 1.8 pad_bitcast_fusion.raw
  2.4 109.0 %forward.1 = (bf16[768,2304]{1,0:T(8,128)(2,1)}, bf16[768,768]{1,0:T(8,128)(2,1)}, bf16[768,3072]{1,0:T(8,128)(2,1)}, bf16[3072,768]{1,0:T(8,128)(2,1)}, bf16[41...) custom-call(bf16[1744,128]{1,0:T(8,128)(2,1)} %pad_bitcast_fusion.ra, ...), custom_call_target="tpu_custom_call" | custom-call | tf_op jit(solution)/shard_map/forward/pallas_call | solution.py:924
  111.4 112.8 %backward.1 = (f32[1744,128]{1,0:T(8,128)}, f32[512,768]{1,0:T(8,128)}) custom-call(bf16[512,768]{1,0:T(8,128)(2,1)} %tokens.3, bf16[512,768]{1,0:T(8,128)(2,1)} %cotangent.1, s32[2,2]{1,0:T(2,128)} %lengths.3, f32[16,3072]{1,0:T(8,128)} %get-tuple-element.20.table, bf16[768,2304]{1,0:T(8,128)(2,1)} %get-tuple-element.21.refs_0_, ...), custom_call_target="tpu_custom_call" | custom-call | tf_op jit(solution)/shard_map/backward/pallas_call | solution.py:2007
  224.2 0.0 copy-start
  224.2 2.3 slice.4
  226.5 2.1 copy.9
  228.5 0.0 copy-done
  228.5 1.1 copy.10
Async XLA Ops:
  224.2 4.3 %copy-start = (f32[512,768]{1,0:T(8,128)S(1)}, f32[512,768]{1,0:T(8,128)}, u32[]{:S(2)}) copy-start(f32[512,768]{1,0:T(8,128)} %get-tuple-element.39) | copy-start | bytes 4718596

commit v3 on v2

--- a/solution.py
+++ b/solution.py
@@ -1319,7 +1319,7 @@
         self.cross_send, self.cross_recv = cross_send, cross_recv
         self.plan = slot_plan(place, 16 * sum(place.shares))
         self.slot, self.sent = 0, []
-        self.waits, self.then, self.left = {}, {}, {}
+        self.waits, self.then = {}, {}
 
     def rect(self, p, k, dest):
         top, high, left, wide = self.parts[p].parts[k]
@@ -1417,7 +1417,6 @@
 
     def offer(self, p, waits, then):
         self.waits[p], self.then[p] = waits, then
-        self.left[p] = len(self.parts[p].parts)
 
     def step(self, p, k, x, y, turn):
         if p in self.waits:
@@ -1427,9 +1426,7 @@
         when(cond, lambda: self.task(p, k, rel, dest))
         self.sent.append((p, k, x, y, turn))
         if x == y == 0 and turn == 4:
-            self.left[p] -= 1
-            if not self.left[p]:
-                self.then[p]()
+            self.then[p](k)
 
     def pump(self):
         self.slot += 1
@@ -1484,25 +1481,34 @@
     def device(d):
         return (quot(d, place.shape[1]), rest(d, place.shape[1]))
 
-    def block_copy(p, block, to, which):
+    def piece(p, k):
+        top, high, left, wide = parts[p].parts[k]
+        return pl.ds(top, high), pl.ds(left, wide)
+
+    def source(p, block, k):
+        top, high, left, wide = parts[p].parts[k]
+        row = pl.multiple_of(block * parts[p].high + top, 16)
+        return own[p].at[core, pl.ds(row, high), pl.ds(left, wide)]
+
+    def block_copy(p, block, to, which, k):
         part = parts[p]
         slot = block - first_block(part, entries, to)
         return pltpu.make_async_remote_copy(
-            src_ref=own[p].at[core, pl.ds(pl.multiple_of(block * part.high, 16), part.high), :],
-            dst_ref=land[p].at[slot, core],
-            send_sem=land_send.at[p, which],
-            recv_sem=land_recv[p].at[slot, core],
+            src_ref=source(p, block, k),
+            dst_ref=land[p].at[slot, core, *piece(p, k)],
+            send_sem=land_send.at[p, which, k],
+            recv_sem=land_recv[p].at[slot, core, k],
             device_id=device(to),
             device_id_type=MESH,
         )
 
-    def block_local(p, block):
+    def block_local(p, block, k):
         part = parts[p]
         slot = block - first_block(part, entries, flat)
         return pltpu.make_async_copy(
-            own[p].at[core, pl.ds(pl.multiple_of(block * part.high, 16), part.high), :],
-            land[p].at[slot, core],
-            local.at[p],
+            source(p, block, k),
+            land[p].at[slot, core, *piece(p, k)],
+            local.at[p, k],
         )
 
     def sends(p):
@@ -1531,11 +1537,11 @@
             device_id_type=MESH,
         )
 
-    def start(p):
+    def start(p, k):
         remote, here = sends(p)
         for cond, to, which in remote:
-            pl.when(cond)(lambda: block_copy(p, mine, to, which).start())
-        pl.when(here)(lambda: block_local(p, mine).start())
+            pl.when(cond)(lambda: block_copy(p, mine, to, which, k).start())
+        pl.when(here)(lambda: block_local(p, mine, k).start())
 
     def start_vectors():
         for n, (block, d) in enumerate(vector_pairs()):
@@ -1569,23 +1575,26 @@
             part = parts[p]
             blocks = 2 * part.half // LANES
             remote, here = sends(p)
-            pl.when(here)(lambda: block_local(p, mine).wait())
+            for k in part.parts:
+                pl.when(here)(lambda: block_local(p, mine, k).wait())
             for cond, block, i in expected(p):
 
                 def take():
                     for half in range(2):
-                        source = place.flat(chip_of_traced(block) + [half])
-
-                        @pl.when(source != flat)
+                        sender = place.flat(chip_of_traced(block) + [half])
+
+                        @pl.when(sender != flat)
                         def _():
-                            pltpu.make_async_remote_copy(
-                                src_ref=land[p].at[i, half],
-                                dst_ref=land[p].at[i, half],
-                                send_sem=land_send.at[p, 0],
-                                recv_sem=land_recv[p].at[i, half],
-                                device_id=device(source),
-                                device_id_type=MESH,
-                            ).wait_recv()
+                            for k in part.parts:
+                                spot = land[p].at[i, half, *piece(p, k)]
+                                pltpu.make_async_remote_copy(
+                                    src_ref=spot,
+                                    dst_ref=spot,
+                                    send_sem=land_send.at[p, 0, k],
+                                    recv_sem=land_recv[p].at[i, half, k],
+                                    device_id=device(sender),
+                                    device_id_type=MESH,
+                                ).wait_recv()
 
                     at = part.low + block * part.rows - base + margin
                     for r in range(part.high // 16):
@@ -1638,7 +1647,8 @@
         loop(rows // 16, merge, 8)
         for p in range(4):
             for cond, to, which in sends(p)[0]:
-                pl.when(cond)(lambda: block_copy(p, mine, to, which).wait_send())
+                for k in parts[p].parts:
+                    pl.when(cond)(lambda: block_copy(p, mine, to, which, k).wait_send())
         for n, (block, d) in enumerate(vector_pairs()):
             home = place.flat(chip_of(block) + [0])
             if home != d:
@@ -1807,7 +1817,7 @@
             adding.swap(p, first, block, i).start()
 
         waits = lambda: loop(steps, lambda i: adding.swap(p, i * block, block, i).wait_recv())
-        adding.offer(p, waits, lambda: start(p))
+        adding.offer(p, waits, lambda k: start(p, k))
         stepped(steps, body, groups)
         swaps.append((p, steps, block))
 
@@ -1980,7 +1990,7 @@
     own[4][0, 0:padded, :] = low(stage[0:padded, :])
     adding.swap(4, 0, parts[4].depth, 0).start()
     swaps.append((4, 1, parts[4].depth))
-    adding.offer(4, lambda: adding.swap(4, 0, parts[4].depth, 0).wait_recv(), start_vectors)
+    adding.offer(4, lambda: adding.swap(4, 0, parts[4].depth, 0).wait_recv(), lambda k: start_vectors())
     adding.pump()
     pieces(W_QKV_NAME, narrow, lambda: wide[:, 0 : 3 * D], 128, 3)
     finish(stage, stage_margin(parts), out)
@@ -2022,13 +2032,13 @@
             pltpu.VMEM((plan[k][1], part.parts[k][1], part.parts[k][3]), bf) for part, k in rects
         ]
         + [dma((plan[k][1],)) for _, k in rects]
-        + [dma((5, place.classes, place.chips)), dma((5, 12)), dma((5, 12)), dma((4, 2))]
-        + [dma((most_blocks(part, entries), 2)) for part in parts[:4]]
+        + [dma((5, place.classes, place.chips)), dma((5, 12)), dma((5, 12)), dma((4, 2, place.classes))]
+        + [dma((most_blocks(part, entries), 2, place.classes)) for part in parts[:4]]
         + [
             pltpu.VMEM((-(-len(VECTOR_LIST) // 16), 16, LANES), bf),
             dma((32,)),
             dma((-(-len(VECTOR_LIST) // 16),)),
-            dma((4,)),
+            dma((4, place.classes)),
             pltpu.VMEM((2 * stage_margin(parts) + rows + 32, LANES), f32),
             pltpu.VMEM(TABLE, f32),
             pltpu.VMEM((FF, D), bf),

time: 230 us -> 231 us (level)
  no operation moved by 1% of the time
where the time goes in v3:
time: 231 us; the launch traced here: 230 us
  Pallas kernels  222 us (96%)
  local copies, waits for them, and re-layouts  7.28 us (3%)
    pallas_call x1, Pallas kernels, even_backward(): pl.pallas_call(functools.partial(even_kernel, place, entries, sz), out_sh...  113 us
    pallas_call x1, Pallas kernels, forward(): pl.pallas_call(functools.partial(forward_kernel, place, entries, sz), out...  109 us

profile of v3, /device:TPU:0, one launch (start us, length us, event | category | flops | bytes accessed | tf_op | source)
XLA Modules:
  0.0 230.3 jit_solution(759699913565300640)
XLA Ops:
  0.6 1.8 pad_bitcast_fusion.raw
  2.4 109.0 %forward.1 = (bf16[768,2304]{1,0:T(8,128)(2,1)}, bf16[768,768]{1,0:T(8,128)(2,1)}, bf16[768,3072]{1,0:T(8,128)(2,1)}, bf16[3072,768]{1,0:T(8,128)(2,1)}, bf16[41...) custom-call(bf16[1744,128]{1,0:T(8,128)(2,1)} %pad_bitcast_fusion.ra, ...), custom_call_target="tpu_custom_call" | custom-call | tf_op jit(solution)/shard_map/forward/pallas_call | solution.py:924
  111.4 113.3 %backward.1 = (f32[1744,128]{1,0:T(8,128)}, f32[512,768]{1,0:T(8,128)}) custom-call(bf16[512,768]{1,0:T(8,128)(2,1)} %tokens.3, bf16[512,768]{1,0:T(8,128)(2,1)} %cotangent.1, s32[2,2]{1,0:T(2,128)} %lengths.3, f32[16,3072]{1,0:T(8,128)} %get-tuple-element.20.table, bf16[768,2304]{1,0:T(8,128)(2,1)} %get-tuple-element.21.refs_0_, ...), custom_call_target="tpu_custom_call" | custom-call | tf_op jit(solution)/shard_map/backward/pallas_call | solution.py:2017
  224.8 0.0 copy-start
  224.8 2.3 slice.4
  227.1 2.1 copy.9
  229.1 0.0 copy-done
  229.1 1.1 copy.10
Async XLA Ops:
  224.8 4.3 %copy-start = (f32[512,768]{1,0:T(8,128)S(1)}, f32[512,768]{1,0:T(8,128)}, u32[]{:S(2)}) copy-start(f32[512,768]{1,0:T(8,128)} %get-tuple-element.39) | copy-start | bytes 4718596

commit v4 on v2

--- a/solution.py
+++ b/solution.py
@@ -1652,41 +1652,41 @@
 
 
 SCHEDULE = (
-        (),
-        (),
-        (),
-        (76, 48, 71),
-        (45,),
-        (75, 70),
-        (55,),
-        (56, 65),
-        (115, 87, 136, 85),
-        (46, 95, 135, 150, 126, 125, 33),
-        (60, 72, 155, 86, 151, 116, 50),
-        (5, 127, 40, 35, 78, 130, 97),
-        (154, 51, 61, 99, 120, 128),
-        (145, 32, 105, 158, 215),
-        (159, 90, 49, 98, 15, 66, 112, 88),
-        (210, 114, 110, 140, 59, 58, 217, 77, 156),
-        (138, 195, 25, 235, 17),
-        (111, 16, 73, 131, 121, 62, 96, 19, 230),
-        (137, 47, 119, 216, 178, 6, 146),
-        (57, 41, 7, 238, 157, 207, 237, 68, 206, 152, 205, 79),
-        (141, 219, 233, 118, 122, 218, 139, 193, 225, 67, 37, 236),
-        (133, 39, 30, 220, 10, 209, 9),
-        (132, 147, 113, 91, 8, 231, 52, 74, 42, 80, 36),
-        (53, 200, 117, 199, 92, 134, 69, 221),
-        (106, 142, 173, 0, 232, 38, 108, 100, 153),
-        (208, 109, 129, 12, 20, 226, 175, 93, 201, 185, 63, 211, 18, 190),
-        (11, 222, 107, 223, 176, 81, 196, 26, 31, 43, 179, 168, 101, 197, 278, 191, 28, 166, 227,
-     310, 277, 256, 212, 13, 255, 228, 198, 257, 82, 295, 258, 273, 275, 234, 271, 296, 1, 123, 313,
-     315, 21, 270, 285, 102, 187, 103, 170, 165, 29, 318, 64, 276, 14, 300, 245, 188, 286, 316, 317,
-     203, 239, 2, 169, 250, 311, 298, 252, 279, 23, 290, 192, 305, 3, 180, 83, 265, 186, 177, 202,
-     171, 27, 251, 160, 89, 280, 291, 248, 148, 297, 306, 194, 260, 172, 167, 319, 259, 94, 247,
-     229, 181, 281, 240, 34, 253, 288, 246, 312, 266, 307, 213, 254, 149, 22, 268, 299, 224, 143,
-     274, 161, 272, 182, 301, 241, 124, 214, 292, 293, 287, 174, 261, 308, 54, 162, 267, 183, 289,
-     189, 249, 24, 163, 283, 269, 302, 84, 303, 242, 104, 314, 144, 282, 243, 204, 309, 294, 262,
-     263, 4, 44, 184, 164, 244, 304, 284, 264),
+    (),
+    (),
+    (55, 78, 70),
+    (),
+    (50, 72, 60),
+    (71, 56, 76),
+    (77, 45, 58),
+    (35, 5, 48, 7),
+    (75, 155, 47, 46, 18),
+    (158, 51, 40, 125, 137, 127, 6),
+    (117, 150, 96, 65, 17, 135, 126, 74),
+    (30, 19, 87, 15),
+    (66, 95, 36, 111, 99),
+    (61, 98, 110, 130, 89, 41),
+    (114, 120, 68, 38, 116, 97, 32, 195, 233, 236, 115, 39, 140, 205, 145),
+    (215, 238, 25, 151, 216),
+    (138, 156, 62, 57, 33, 90, 8, 31, 37, 136, 85, 93, 105, 206, 235),
+    (129, 67, 210, 153, 121, 196, 88),
+    (146, 152, 200, 185, 157, 29, 113),
+    (217, 191, 91, 207, 179, 141),
+    (20, 52, 122, 73, 100, 197, 118, 59, 168, 92),
+    (53, 79, 9, 211, 154, 106, 139, 131),
+    (13, 94, 147, 230, 16, 128, 42, 80, 28, 49, 10, 26, 201, 86),
+    (132, 178, 190, 159, 133, 208, 212, 225, 142),
+    (69, 218, 231, 11, 108, 220, 232, 112, 0, 119, 107),
+    (54, 81, 237, 63, 202, 175, 226, 186, 101),
+    (1, 166, 199, 12, 193, 176, 198, 228, 165, 239, 221, 177, 298, 248, 278, 187, 123, 180, 21,
+     170, 313, 64, 173, 310, 255, 227, 295, 245, 143, 285, 82, 315, 102, 174, 256, 172, 258,
+     257, 2, 171, 275, 296, 276, 288, 316, 188, 181, 270, 160, 219, 203, 250, 192, 300, 305,
+     290, 148, 318, 83, 109, 277, 161, 222, 311, 265, 134, 189, 43, 317, 167, 253, 149, 271,
+     306, 266, 297, 163, 103, 246, 223, 280, 247, 268, 84, 213, 251, 291, 240, 169, 44, 312,
+     286, 3, 259, 14, 260, 252, 272, 27, 209, 229, 301, 267, 194, 144, 104, 273, 124, 307, 182,
+     23, 299, 292, 279, 241, 287, 308, 293, 162, 183, 34, 214, 261, 281, 249, 319, 234, 22, 243,
+     302, 289, 274, 4, 164, 269, 303, 314, 204, 254, 283, 262, 294, 242, 184, 309, 282, 224,
+     263, 24, 244, 304, 264, 284),
 )
 TURNS = ((3, 2, 1, 3, 0), (3, 3, 2, 0, 1))
 

time: 230 us -> 228 us (level)
  no operation moved by 1% of the time
where the time goes in v4:
time: 228 us
  Pallas kernels  220 us (96%)
  local copies, waits for them, and re-layouts  7.28 us (3%)
    pallas_call x1, Pallas kernels, even_backward(): pl.pallas_call(functools.partial(even_kernel, place, entries, sz), out_sh...  111 us
    pallas_call x1, Pallas kernels, forward(): pl.pallas_call(functools.partial(forward_kernel, place, entries, sz), out...  109 us

profile of v4, /device:TPU:0, one launch (start us, length us, event | category | flops | bytes accessed | tf_op | source)
XLA Modules:
  0.0 228.0 jit_solution(7547823513561372224)
XLA Ops:
  0.6 1.8 pad_bitcast_fusion.raw
  2.4 109.0 %forward.1 = (bf16[768,2304]{1,0:T(8,128)(2,1)}, bf16[768,768]{1,0:T(8,128)(2,1)}, bf16[768,3072]{1,0:T(8,128)(2,1)}, bf16[3072,768]{1,0:T(8,128)(2,1)}, bf16[41...) custom-call(bf16[1744,128]{1,0:T(8,128)(2,1)} %pad_bitcast_fusion.ra, ...), custom_call_target="tpu_custom_call" | custom-call | tf_op jit(solution)/shard_map/forward/pallas_call | solution.py:924
  111.4 111.0 %backward.1 = (f32[1744,128]{1,0:T(8,128)}, f32[512,768]{1,0:T(8,128)}) custom-call(bf16[512,768]{1,0:T(8,128)(2,1)} %tokens.3, bf16[512,768]{1,0:T(8,128)(2,1)} %cotangent.1, s32[2,2]{1,0:T(2,128)} %lengths.3, f32[16,3072]{1,0:T(8,128)} %get-tuple-element.20.table, bf16[768,2304]{1,0:T(8,128)(2,1)} %get-tuple-element.21.refs_0_, ...), custom_call_target="tpu_custom_call" | custom-call | tf_op jit(solution)/shard_map/backward/pallas_call | solution.py:2007
  222.5 0.0 copy-start
  222.5 2.3 slice.4
  224.8 2.1 copy.9
  226.8 0.0 copy-done
  226.8 1.1 copy.10
Async XLA Ops:
  222.5 4.3 %copy-start = (f32[512,768]{1,0:T(8,128)S(1)}, f32[512,768]{1,0:T(8,128)}, u32[]{:S(2)}) copy-start(f32[512,768]{1,0:T(8,128)} %get-tuple-element.39) | copy-start | bytes 4718596
